TPU v7x, 512 devices: a whole 4x4x16 slice. The times are simulated.
512 devices in a mesh: row: 16 (over x, y_hi, core), col: 32 (over y_lo, z).
Axes of the slice: x: 4, y: 4 (y_hi: 2, y_lo: 2; y = y_hi * 2 + y_lo), z: 16, core: 2. Of those that a mesh axis runs over, the one named last changes fastest.
Arguments:
- contact: bfloat16 [1024, 65536], P('row', 'col'), may hold values from -6 to 6
- first_down: bfloat16 [2, 3, 3, 32, 64], replicated, may hold values from -0.25 to 0.25
- first_down_bias: float32 [2, 32], replicated, may hold values from -1.5 to 1.5
- first_up: bfloat16 [2, 3, 3, 64, 32], replicated, may hold values from -0.375 to 0.375
- first_up_bias: float32 [2, 64], replicated, may hold values from -1.5 to 1.5
- second_down: bfloat16 [2, 3, 3, 32, 64], replicated, may hold values from -0.25 to 0.25
- second_down_bias: float32 [2, 32], replicated, may hold values from -1.5 to 1.5
- second_up: bfloat16 [2, 3, 3, 64, 32], replicated, may hold values from -0.375 to 0.375
- second_up_bias: float32 [2, 64], replicated, may hold values from -1.5 to 1.5
Outputs:
- decoded: bfloat16 [1024, 65536], P('row', 'col')
All inputs are finite; a program needn't handle non-finite values.
Results may differ from a plain program's by a relative error of at most 0.012.
Values may be sent and summed in bfloat16 or wider, within the bound.
No kernel may reach another device: no remote copies, remote signals or barrier semaphores. Data moves between devices by JAX's collectives and lax.ppermute only.
A program may use at most 64 MiB of HBM per device.

v0:
```python
import functools

import jax
import jax.numpy as jnp
from jax import lax
from jax.experimental import pallas as pl
from jax.experimental.pallas import tpu as pltpu
from jax.sharding import PartitionSpec as P

ROWS = 64
COLS = 32
CH = 64
HALO = 16
TALL = ROWS + 2 * HALO
F32 = jnp.float32
BF16 = jnp.bfloat16


def lane_group(width, rows):
    return lax.broadcasted_iota(jnp.int32, (rows, 128), 1) // width


def build_weights(down, up, w1, w2, w3, w4):
    by32 = lane_group(32, 64)
    by64 = lane_group(64, 32)
    zero_down = jnp.zeros((64, 128), BF16)
    zero_up = jnp.zeros((32, 128), BF16)
    for p in range(3):
        for i in range(8):
            block = zero_down
            for q in range(3):
                o = i - 1 - q
                if 0 <= o < 4:
                    block = jnp.where(by32 == o, down[0, p, q], block)
            w1[i * 64 : (i + 1) * 64, p * 128 : (p + 1) * 128] = block
        for i in range(8):
            for half in range(2):
                block = zero_up
                for q in range(3):
                    o = i - 2 * q
                    if 0 <= o < 4 and o // 2 == half:
                        block = jnp.where(by64 == o % 2, up[0, p, q], block)
                w2[i * 32 : (i + 1) * 32, p * 256 + half * 128 : p * 256 + half * 128 + 128] = block
        for t in range(4):
            for e in range(2):
                block = zero_down
                for u in range(2):
                    q = t - u
                    if 0 <= q < 3:
                        block = jnp.where(by32 == 2 * u + e, down[1, p, q], block)
                w3[t * 128 + e * 64 : t * 128 + e * 64 + 64, p * 128 : (p + 1) * 128] = block
        for q in range(3):
            for g in range(4):
                for half in range(2):
                    block = zero_up
                    if g // 2 == half:
                        block = jnp.where(by64 == g % 2, up[1, p, q], block)
                    w4[
                        q * 128 + g * 32 : q * 128 + g * 32 + 32,
                        p * 256 + half * 128 : p * 256 + half * 128 + 128,
                    ] = block


def section_kernel(
    size, at, own, left, right, above, below, down, down_bias, up, up_bias, out,
    v, h1, h2, w1, w2, w3, w4, row_mask
):
    build_weights(down, up, w1, w2, w3, w4)
    row0, col0 = at[0], at[1]
    height, width = size

    rows = row0 + lax.broadcasted_iota(jnp.int32, (TALL, 128), 0)
    row_mask[...] = ((rows >= 0) & (rows < height)).astype(F32)
    v[0] = jnp.zeros((TALL, 128), BF16)
    v[33] = jnp.zeros((TALL, 128), BF16)
    for i in range(32):
        lanes = slice(i * 128, (i + 1) * 128)
        v[i + 1, 0:HALO, :] = above[:, lanes]
        v[i + 1, HALO + ROWS : TALL, :] = below[:, lanes]
        if i < 8:
            middle = left[:, lanes]
        elif i < 24:
            middle = own[:, (i - 8) * 128 : (i - 7) * 128]
        else:
            middle = right[:, (i - 24) * 128 : (i - 23) * 128]
        v[i + 1, HALO : HALO + ROWS, :] = middle

    lane32 = lane_group(32, 1)
    lane64 = lane_group(64, 1)

    def col_mask(cols):
        return ((cols >= 0) & (cols < width)).astype(F32)

    def wide_dot(chunks, w):
        lhs = jnp.concatenate([jnp.concatenate(c, axis=0) for c in chunks], axis=1)
        return jnp.dot(lhs, w[...], preferred_element_type=F32)

    def taps(res, g, d, lo, n):
        part = res[g * TALL : (g + 1) * TALL]
        top = part[:, lo : lo + 128]
        mid = part[:, n + lo : n + lo + 128]
        low = part[:, 2 * n + lo : 2 * n + lo + 128]
        return pltpu.roll(top, d, 0) + mid + pltpu.roll(low, TALL - d, 0)

    def first_down(jj, _):
        j0 = jj * 4
        res = wide_dot([[v[2 * (j0 + g) + t] for g in range(4)] for t in range(4)], w1)
        for g in range(4):
            hidden = jnp.maximum(taps(res, g, 1, 0, 128) + down_bias[0:1], 0.0)
            keep = col_mask(col0 + 4 * (j0 + g) + lane32)
            h1[j0 + g] = (hidden * row_mask[...] * keep).astype(BF16)
        return 0

    lax.fori_loop(0, 4, first_down, 0)

    def first_up(kk, _):
        k0 = kk * 3
        res = wide_dot([[h1[k0 + g + t] for g in range(3)] for t in range(2)], w2)
        for g in range(3):
            for half in range(2):
                i = 2 * (k0 + g) + 1 + half
                update = taps(res, g, 2, half * 128, 256) + up_bias[0:1]
                value = (v[i + 1].astype(F32) + update) * row_mask[...]
                v[i + 1] = (value * col_mask(col0 + 2 * i + lane64)).astype(BF16)
        return 0

    lax.fori_loop(0, 5, first_up, 0)

    def second_down(mm, _):
        groups = [(1 + 2 * mm + dm, s) for dm in range(2) for s in range(2)]
        res = wide_dot([[v[4 * m + s - 1 + 2 * t] for m, s in groups] for t in range(4)], w3)
        for g, (m, s) in enumerate(groups):
            hidden = jnp.maximum(taps(res, g, 4, 0, 128) + down_bias[1:2], 0.0)
            keep = col_mask(col0 + 8 * m + 2 * s + 4 * (lane32 // 2) + lane32 % 2)
            h2[2 * (m - 1) + s] = (hidden * row_mask[...] * keep).astype(BF16)
        return 0

    lax.fori_loop(0, 3, second_down, 0)

    def second_up(mm, _):
        groups = [(2 + 2 * mm + dm, s) for dm in range(2) for s in range(2)]
        res = wide_dot([[h2[2 * (m - 2 + q) + s] for m, s in groups] for q in range(3)], w4)
        for g, (m, s) in enumerate(groups):
            base = g * TALL
            for half in range(2):
                lo = half * 128
                update = (
                    res[base + 8 : base + 72, lo : lo + 128]
                    + res[base + 16 : base + 80, 256 + lo : 384 + lo]
                    + res[base + 24 : base + 88, 512 + lo : 640 + lo]
                    + up_bias[1:2]
                )
                i = 4 * m + s + 2 * half
                value = v[i + 1][HALO : HALO + ROWS].astype(F32) + update
                at_lane = pl.multiple_of((i - 8) * 128, 128)
                out[:, pl.ds(at_lane, 128)] = value.astype(BF16)
        return 0

    lax.fori_loop(0, 2, second_up, 0)


def section(size, at, pieces, down, down_bias, up, up_bias):
    vmem = pl.BlockSpec(memory_space=pltpu.VMEM)
    return pl.pallas_call(
        functools.partial(section_kernel, size),
        out_shape=jax.ShapeDtypeStruct((ROWS, COLS * CH), BF16),
        in_specs=[pl.BlockSpec(memory_space=pltpu.SMEM)] + [vmem] * 9,
        out_specs=vmem,
        scratch_shapes=[
            pltpu.VMEM((34, TALL, 128), BF16),
            pltpu.VMEM((16, TALL, 128), BF16),
            pltpu.VMEM((12, TALL, 128), BF16),
            pltpu.VMEM((512, 384), BF16),
            pltpu.VMEM((256, 768), BF16),
            pltpu.VMEM((512, 384), BF16),
            pltpu.VMEM((384, 768), BF16),
            pltpu.VMEM((TALL, 128), F32),
        ],
        compiler_params=pltpu.CompilerParams(vmem_limit_bytes=32 << 20),
    )(at, *pieces, down, down_bias, up, up_bias)


def solution(mesh):
    row_count, col_count = mesh.shape["row"], mesh.shape["col"]
    size = (row_count * ROWS, col_count * COLS)
    flip = row_count // 4
    axes = ("row", "col")

    def send(x, target):
        pairs = []
        for r in range(row_count):
            for c in range(col_count):
                to = target(r, c)
                if 0 <= to[0] < row_count and 0 <= to[1] < col_count:
                    pairs.append((r * col_count + c, to[0] * col_count + to[1]))
        return lax.ppermute(x, axes, pairs)

    def with_rim(x):
        depth = HALO * CH
        right = send(x[:, :depth], lambda r, c: (r, c - 1))
        left = send(x[:, -depth:], lambda r, c: (r, c + 1))
        wide = jnp.concatenate([left[:HALO], x[:HALO], right[:HALO]], axis=1)
        wide_low = jnp.concatenate([left[-HALO:], x[-HALO:], right[-HALO:]], axis=1)
        below = send(wide, lambda r, c: (r - 1, c))
        above = send(wide_low, lambda r, c: (r + 1, c))
        return x, left, right, above, below

    def mirrored(x, parity):
        turned = x.reshape(2, 32, 32, CH).transpose(0, 2, 1, 3).reshape(2, 32, 32 * CH)
        near = lax.dynamic_index_in_dim(turned, parity, 0, keepdims=False)
        far = lax.dynamic_index_in_dim(turned, 1 - parity, 0, keepdims=False)
        far = send(far, lambda r, c: (r ^ flip, c))
        near = send(near, lambda r, c: (c // 2, 2 * r + c % 2))
        far = send(far, lambda r, c: (c // 2, 2 * (r ^ flip) + 1 - c % 2))
        even = jnp.concatenate([near, far], axis=0)
        odd = jnp.concatenate([far, near], axis=0)
        return jnp.where(parity == 0, even, odd)

    def per_device(contact, d1, db1, u1, ub1, d2, db2, u2, ub2):
        row, col = lax.axis_index("row"), lax.axis_index("col")
        at = jnp.stack([row * ROWS - HALO, col * COLS - HALO]).astype(jnp.int32)

        def prepared(down, down_bias, up, up_bias):
            return (
                jnp.tile(down.transpose(0, 1, 2, 4, 3), (1, 1, 1, 1, 4)),
                jnp.tile(down_bias, (1, 4)),
                jnp.tile(up.transpose(0, 1, 2, 4, 3), (1, 1, 1, 1, 2)),
                jnp.tile(up_bias, (1, 2)),
            )

        first = section(size, at, with_rim(contact), *prepared(d1, db1, u1, ub1))
        flipped = mirrored(first, col % 2)
        symmetric = ((first.astype(F32) + flipped.astype(F32)) * 0.5).astype(BF16)
        return section(size, at, with_rim(symmetric), *prepared(d2, db2, u2, ub2))

    in_specs = (P("row", "col"), P(), P(), P(), P(), P(), P(), P(), P())
    return jax.shard_map(
        per_device, mesh=mesh, in_specs=in_specs, out_specs=P("row", "col"), check_vma=False
    )
```

profile of v0, /device:TPU:12, one launch (start us, length us, event | category | flops | bytes accessed | tf_op | source)
XLA Modules:
  0.0 100.9 jit_solution(415838506050683970)
XLA Ops:
  0.0 1.0 %fusion.3 = (bf16[64,1024]{1,0:T(8,128)(2,1)S(1)}, bf16[64,1024]{1,0:T(8,128)(2,1)S(1)}) fusion(bf16[64,2048]{1,0:T(8,128)(2,1)} %own.1), kind=kLoop, calls=%fused_computation.12 | loop fusion | bytes 524288 | tf_op jit(solution)/shard_map/slice | solution.py:200
  1.0 3.8 %collective-permute-start = (bf16[64,1024]{1,0:T(8,128)(2,1)S(1)}, bf16[64,1024]{1,0:T(8,128)(2,1)S(1)}, u32[]{:S(2)}, u32[]{:S(2)}) collective-permute-start(bf16[64,1024]{1,0:T(8,128)(2,1)S(1)} %get-tuple-element.14), channel_id=1, source_target_pairs={{0,1},{1,2},{2,3},{3,4},{4,5},{5,6},{6,7},{7,8},{8,9},{9,10},{10,1... | collective-permute-start | bytes 393224 | tf_op jit(solution)/shard_map/ppermute | solution.py:196
  4.9 9.4 %collective-permute-start.1 = (bf16[64,1024]{1,0:T(8,128)(2,1)S(1)}, bf16[64,1024]{1,0:T(8,128)(2,1)S(1)}, u32[]{:S(2)}, u32[]{:S(2)}) collective-permute-start(bf16[64,1024]{1,0:T(8,128)(2,1)S(1)} %get-tuple-element.13), channel_id=1, source_target_pairs={{1,0},{2,1},{3,2},{4,3},{5,4},{6,5},{7,6},{8,7},{9,8},{10,9},{11,1... | collective-permute-start | bytes 393224 | tf_op jit(solution)/shard_map/ppermute | solution.py:196
  14.3 1.5 %collective-permute-done.left = bf16[64,1024]{1,0:T(8,128)(2,1)S(1)} collective-permute-done((bf16[64,1024]{1,0:T(8,128)(2,1)S(1)}, bf16[64,1024]{1,0:T(8,128)(2,1)S(1)}, u32[]{:S(2)}, u32[]{:S(2)}) %collective-permute-start) | collective-permute-done | bytes 131104 | tf_op jit(solution)/shard_map/ppermute | solution.py:196
  15.8 1.2 %collective-permute-done.1.right = bf16[64,1024]{1,0:T(8,128)(2,1)S(1)} collective-permute-done((bf16[64,1024]{1,0:T(8,128)(2,1)S(1)}, bf16[64,1024]{1,0:T(8,128)(2,1)S(1)}, u32[]{:S(2)}, u32[]{:S(2)}) %collective-permute-start.1) | collective-permute-done | bytes 131104 | tf_op jit(solution)/shard_map/ppermute | solution.py:196
  17.0 3.1 %collective-permute-start.3 = (bf16[16,4096]{1,0:T(8,128)(2,1)S(1)}, bf16[16,4096]{1,0:T(8,128)(2,1)S(1)}, u32[]{:S(2)}, u32[]{:S(2)}) collective-permute-start(bf16[16,4096]{1,0:T(8,128)(2,1)S(1)} %pad_maximum_fusion.1), channel_id=1, source_target_pairs={{32,0},{33,1},{34,2},{35,3},{36,4},{37,5},{38,6},{39,7},{40,8},{41... | collective-permute-start | bytes 393224 | tf_op jit(solution)/shard_map/ppermute | solution.py:196
  20.1 2.1 %collective-permute-start.2 = (bf16[16,4096]{1,0:T(8,128)(2,1)S(1)}, bf16[16,4096]{1,0:T(8,128)(2,1)S(1)}, u32[]{:S(2)}, u32[]{:S(2)}) collective-permute-start(bf16[16,4096]{1,0:T(8,128)(2,1)S(1)} %pad_maximum_fusion), channel_id=1, source_target_pairs={{0,32},{1,33},{2,34},{3,35},{4,36},{5,37},{6,38},{7,39},{8,40},{9,... | collective-permute-start | bytes 393224 | tf_op jit(solution)/shard_map/ppermute | solution.py:196
  22.3 0.3 copy.13.down
  22.6 0.6 copy-done.1
  23.6 0.5 copy-done.5
  24.2 0.6 copy-done.6
  25.0 4.0 %collective-permute-done.2.above = bf16[16,4096]{1,0:T(8,128)(2,1)S(1)} collective-permute-done((bf16[16,4096]{1,0:T(8,128)(2,1)S(1)}, bf16[16,4096]{1,0:T(8,128)(2,1)S(1)}, u32[]{:S(2)}, u32[]{:S(2)}) %collective-permute-start.2) | collective-permute-done | bytes 131104 | tf_op jit(solution)/shard_map/ppermute | solution.py:196
  28.9 6.0 %shard_map.91 = bf16[64,2048]{1,0:T(8,128)(2,1)S(1)} custom-call(s32[2]{0:T(128)S(1)} %pad_add_fusion.at, bf16[64,2048]{1,0:T(8,128)(2,1)S(1)} %copy-done, bf16[64,1024]{1,0:T(8,128)(2,1)S(1)} %collective-permute-done.left, bf16[64,1024]{1,0:T(8,128)(2,1)S(1)} %collective-permute-done.1.right, bf16[16,4096]{1,0:T(8,128)(2,1)S(1)} %collective-permute-done.2.above, ...), custom_call_target="tpu_custom_call" | custom-call | tf_op jit(solution)/shard_map/pallas_call | solution.py:164
  35.0 0.5 reshape.38
  35.7 0.5 reshape.39
  36.2 3.4 %collective-permute-start.5 = (bf16[32,2048]{1,0:T(8,128)(2,1)S(1)}, bf16[32,2048]{1,0:T(8,128)(2,1)S(1)}, u32[]{:S(2)}, u32[]{:S(2)}) collective-permute-start(bf16[32,2048]{1,0:T(8,128)(2,1)S(1)} %get-tuple-element.10), channel_id=1, source_target_pairs={{0,128},{1,129},{2,130},{3,131},{4,132},{5,133},{6,134},{7,135},{8... | collective-permute-start | bytes 393224 | tf_op jit(solution)/shard_map/ppermute | solution.py:196
  39.6 0.7 collective-permute-start.4
  40.3 2.8 %collective-permute-done.5 = bf16[32,2048]{1,0:T(8,128)(2,1)S(1)} collective-permute-done((bf16[32,2048]{1,0:T(8,128)(2,1)S(1)}, bf16[32,2048]{1,0:T(8,128)(2,1)S(1)}, u32[]{:S(2)}, u32[]{:S(2)}) %collective-permute-start.5) | collective-permute-done | bytes 131104 | tf_op jit(solution)/shard_map/ppermute | solution.py:196
  43.0 8.2 %collective-permute-start.6 = (bf16[32,2048]{1,0:T(8,128)(2,1)S(1)}, bf16[32,2048]{1,0:T(8,128)(2,1)S(1)}, u32[]{:S(2)}, u32[]{:S(2)}) collective-permute-start(bf16[32,2048]{1,0:T(8,128)(2,1)S(1)} %collective-permute-done.5), channel_id=1, source_target_pairs={{0,9},{1,8},{2,41},{3,40},{4,73},{5,72},{6,105},{7,104},{8,137},{9... | collective-permute-start | bytes 393224 | tf_op jit(solution)/shard_map/ppermute | solution.py:196
  51.3 6.3 %collective-permute-done.6 = bf16[32,2048]{1,0:T(8,128)(2,1)S(1)} collective-permute-done((bf16[32,2048]{1,0:T(8,128)(2,1)S(1)}, bf16[32,2048]{1,0:T(8,128)(2,1)S(1)}, u32[]{:S(2)}, u32[]{:S(2)}) %collective-permute-start.6) | collective-permute-done | bytes 131104 | tf_op jit(solution)/shard_map/ppermute | solution.py:196
  57.7 11.7 %collective-permute-start.7 = (bf16[64,1024]{1,0:T(8,128)(2,1)S(1)}, bf16[64,1024]{1,0:T(8,128)(2,1)S(1)}, u32[]{:S(2)}, u32[]{:S(2)}) collective-permute-start(bf16[64,1024]{1,0:T(8,128)(2,1)S(1)} %get-tuple-element.8), channel_id=1, source_target_pairs={{0,1},{1,2},{2,3},{3,4},{4,5},{5,6},{6,7},{7,8},{8,9},{9,10},{10,1... | collective-permute-start | bytes 393224 | tf_op jit(solution)/shard_map/ppermute | solution.py:196
  69.5 8.0 %collective-permute-start.8 = (bf16[64,1024]{1,0:T(8,128)(2,1)S(1)}, bf16[64,1024]{1,0:T(8,128)(2,1)S(1)}, u32[]{:S(2)}, u32[]{:S(2)}) collective-permute-start(bf16[64,1024]{1,0:T(8,128)(2,1)S(1)} %get-tuple-element.7), channel_id=1, source_target_pairs={{1,0},{2,1},{3,2},{4,3},{5,4},{6,5},{7,6},{8,7},{9,8},{10,9},{11,1... | collective-permute-start | bytes 393224 | tf_op jit(solution)/shard_map/ppermute | solution.py:196
  77.5 1.0 collective-permute-done.7.left
  78.5 1.5 %collective-permute-done.8.right = bf16[64,1024]{1,0:T(8,128)(2,1)S(1)} collective-permute-done((bf16[64,1024]{1,0:T(8,128)(2,1)S(1)}, bf16[64,1024]{1,0:T(8,128)(2,1)S(1)}, u32[]{:S(2)}, u32[]{:S(2)}) %collective-permute-start.8) | collective-permute-done | bytes 131104 | tf_op jit(solution)/shard_map/ppermute | solution.py:196
  80.1 5.4 %collective-permute-start.10 = (bf16[16,4096]{1,0:T(8,128)(2,1)S(1)}, bf16[16,4096]{1,0:T(8,128)(2,1)S(1)}, u32[]{:S(2)}, u32[]{:S(2)}) collective-permute-start(bf16[16,4096]{1,0:T(8,128)(2,1)S(1)} %pad_maximum_fusion.3), channel_id=1, source_target_pairs={{32,0},{33,1},{34,2},{35,3},{36,4},{37,5},{38,6},{39,7},{40,8},{41... | collective-permute-start | bytes 393224 | tf_op jit(solution)/shard_map/ppermute | solution.py:196
  85.4 1.9 %collective-permute-start.9 = (bf16[16,4096]{1,0:T(8,128)(2,1)S(1)}, bf16[16,4096]{1,0:T(8,128)(2,1)S(1)}, u32[]{:S(2)}, u32[]{:S(2)}) collective-permute-start(bf16[16,4096]{1,0:T(8,128)(2,1)S(1)} %pad_maximum_fusion.2), channel_id=1, source_target_pairs={{0,32},{1,33},{2,34},{3,35},{4,36},{5,37},{6,38},{7,39},{8,40},{9,... | collective-permute-start | bytes 393224 | tf_op jit(solution)/shard_map/ppermute | solution.py:196
  87.5 0.3 copy.15.down
  87.8 0.6 copy-done.2
  88.8 0.5 copy-done.7
  89.4 0.6 copy-done.8
  90.1 4.1 %collective-permute-done.9.above = bf16[16,4096]{1,0:T(8,128)(2,1)S(1)} collective-permute-done((bf16[16,4096]{1,0:T(8,128)(2,1)S(1)}, bf16[16,4096]{1,0:T(8,128)(2,1)S(1)}, u32[]{:S(2)}, u32[]{:S(2)}) %collective-permute-start.9) | collective-permute-done | bytes 131104 | tf_op jit(solution)/shard_map/ppermute | solution.py:196
  94.1 6.7 %shard_map.92 = bf16[64,2048]{1,0:T(8,128)(2,1)} custom-call(s32[2]{0:T(128)S(1)} %pad_add_fusion.at, bf16[64,2048]{1,0:T(8,128)(2,1)S(1)} %multiply_convert_fusion.own, bf16[64,1024]{1,0:T(8,128)(2,1)S(1)} %collective-permute-done.7.left, bf16[64,1024]{1,0:T(8,128)(2,1)S(1)} %collective-permute-done.8.right, ...), custom_call_target="tpu_custom_call" | custom-call | tf_op jit(solution)/shard_map/pallas_call | solution.py:164
  (44 shorter events, 1.8 us)
Async XLA Ops:
  0.0 14.3 %copy-start = (bf16[64,2048]{1,0:T(8,128)(2,1)S(1)}, bf16[64,2048]{1,0:T(8,128)(2,1)}, u32[]{:S(2)}) copy-start(bf16[64,2048]{1,0:T(8,128)(2,1)} %own.1) | copy-start | bytes 786436
  1.0 14.8 %collective-permute-start = (bf16[64,1024]{1,0:T(8,128)(2,1)S(1)}, bf16[64,1024]{1,0:T(8,128)(2,1)S(1)}, u32[]{:S(2)}, u32[]{:S(2)}) collective-permute-start(bf16[64,1024]{1,0:T(8,128)(2,1)S(1)} %get-tuple-element.14), channel_id=1, source_target_pairs={{0,1},{1,2},{2,3},{3,4},{4,5},{5,6},{6,7},{7,8},{8,9},{9,10},{10,1... | collective-permute-start | bytes 393224 | tf_op jit(solution)/shard_map/ppermute | solution.py:196
  4.9 12.1 %collective-permute-start.1 = (bf16[64,1024]{1,0:T(8,128)(2,1)S(1)}, bf16[64,1024]{1,0:T(8,128)(2,1)S(1)}, u32[]{:S(2)}, u32[]{:S(2)}) collective-permute-start(bf16[64,1024]{1,0:T(8,128)(2,1)S(1)} %get-tuple-element.13), channel_id=1, source_target_pairs={{1,0},{2,1},{3,2},{4,3},{5,4},{6,5},{7,6},{8,7},{9,8},{10,9},{11,1... | collective-permute-start | bytes 393224 | tf_op jit(solution)/shard_map/ppermute | solution.py:196
  17.0 8.0 %collective-permute-start.3 = (bf16[16,4096]{1,0:T(8,128)(2,1)S(1)}, bf16[16,4096]{1,0:T(8,128)(2,1)S(1)}, u32[]{:S(2)}, u32[]{:S(2)}) collective-permute-start(bf16[16,4096]{1,0:T(8,128)(2,1)S(1)} %pad_maximum_fusion.1), channel_id=1, source_target_pairs={{32,0},{33,1},{34,2},{35,3},{36,4},{37,5},{38,6},{39,7},{40,8},{41... | collective-permute-start | bytes 393224 | tf_op jit(solution)/shard_map/ppermute | solution.py:196
  20.1 2.1 %copy-start.3 = (bf16[2,3,3,32,64]{4,3,2,1,0:T(8,128)(2,1)S(1)}, bf16[2,3,3,32,64]{4,3,2,1,0:T(8,128)(2,1)}, u32[]{:S(2)}) copy-start(bf16[2,3,3,32,64]{4,3,2,1,0:T(8,128)(2,1)} %param.10) | copy-start | bytes 221188
  20.1 8.8 %collective-permute-start.2 = (bf16[16,4096]{1,0:T(8,128)(2,1)S(1)}, bf16[16,4096]{1,0:T(8,128)(2,1)S(1)}, u32[]{:S(2)}, u32[]{:S(2)}) collective-permute-start(bf16[16,4096]{1,0:T(8,128)(2,1)S(1)} %pad_maximum_fusion), channel_id=1, source_target_pairs={{0,32},{1,33},{2,34},{3,35},{4,36},{5,37},{6,38},{7,39},{8,40},{9,... | collective-permute-start | bytes 393224 | tf_op jit(solution)/shard_map/ppermute | solution.py:196
  22.3 0.9 copy-start.1
  23.4 0.7 copy-start.5
  24.1 0.7 copy-start.6
  36.2 6.9 %collective-permute-start.5 = (bf16[32,2048]{1,0:T(8,128)(2,1)S(1)}, bf16[32,2048]{1,0:T(8,128)(2,1)S(1)}, u32[]{:S(2)}, u32[]{:S(2)}) collective-permute-start(bf16[32,2048]{1,0:T(8,128)(2,1)S(1)} %get-tuple-element.10), channel_id=1, source_target_pairs={{0,128},{1,129},{2,130},{3,131},{4,132},{5,133},{6,134},{7,135},{8... | collective-permute-start | bytes 393224 | tf_op jit(solution)/shard_map/ppermute | solution.py:196
  39.6 11.7 %collective-permute-start.4 = (bf16[32,2048]{1,0:T(8,128)(2,1)S(1)}, bf16[32,2048]{1,0:T(8,128)(2,1)S(1)}, u32[]{:S(2)}, u32[]{:S(2)}) collective-permute-start(bf16[32,2048]{1,0:T(8,128)(2,1)S(1)} %get-tuple-element.9), channel_id=1, source_target_pairs={{0,0},{1,1},{2,32},{3,33},{4,64},{5,65},{6,96},{7,97},{8,128},{9,1... | collective-permute-start | bytes 393224 | tf_op jit(solution)/shard_map/ppermute | solution.py:196
  43.0 14.6 %collective-permute-start.6 = (bf16[32,2048]{1,0:T(8,128)(2,1)S(1)}, bf16[32,2048]{1,0:T(8,128)(2,1)S(1)}, u32[]{:S(2)}, u32[]{:S(2)}) collective-permute-start(bf16[32,2048]{1,0:T(8,128)(2,1)S(1)} %collective-permute-done.5), channel_id=1, source_target_pairs={{0,9},{1,8},{2,41},{3,40},{4,73},{5,72},{6,105},{7,104},{8,137},{9... | collective-permute-start | bytes 393224 | tf_op jit(solution)/shard_map/ppermute | solution.py:196
  57.7 20.8 %collective-permute-start.7 = (bf16[64,1024]{1,0:T(8,128)(2,1)S(1)}, bf16[64,1024]{1,0:T(8,128)(2,1)S(1)}, u32[]{:S(2)}, u32[]{:S(2)}) collective-permute-start(bf16[64,1024]{1,0:T(8,128)(2,1)S(1)} %get-tuple-element.8), channel_id=1, source_target_pairs={{0,1},{1,2},{2,3},{3,4},{4,5},{5,6},{6,7},{7,8},{8,9},{9,10},{10,1... | collective-permute-start | bytes 393224 | tf_op jit(solution)/shard_map/ppermute | solution.py:196
  69.5 10.5 %collective-permute-start.8 = (bf16[64,1024]{1,0:T(8,128)(2,1)S(1)}, bf16[64,1024]{1,0:T(8,128)(2,1)S(1)}, u32[]{:S(2)}, u32[]{:S(2)}) collective-permute-start(bf16[64,1024]{1,0:T(8,128)(2,1)S(1)} %get-tuple-element.7), channel_id=1, source_target_pairs={{1,0},{2,1},{3,2},{4,3},{5,4},{6,5},{7,6},{8,7},{9,8},{10,9},{11,1... | collective-permute-start | bytes 393224 | tf_op jit(solution)/shard_map/ppermute | solution.py:196
  80.0 7.3 %copy-start.4 = (bf16[2,3,3,32,64]{4,3,2,1,0:T(8,128)(2,1)S(1)}, bf16[2,3,3,32,64]{4,3,2,1,0:T(8,128)(2,1)}, u32[]{:S(2)}) copy-start(bf16[2,3,3,32,64]{4,3,2,1,0:T(8,128)(2,1)} %param.14) | copy-start | bytes 221188
  80.1 10.0 %collective-permute-start.10 = (bf16[16,4096]{1,0:T(8,128)(2,1)S(1)}, bf16[16,4096]{1,0:T(8,128)(2,1)S(1)}, u32[]{:S(2)}, u32[]{:S(2)}) collective-permute-start(bf16[16,4096]{1,0:T(8,128)(2,1)S(1)} %pad_maximum_fusion.3), channel_id=1, source_target_pairs={{32,0},{33,1},{34,2},{35,3},{36,4},{37,5},{38,6},{39,7},{40,8},{41... | collective-permute-start | bytes 393224 | tf_op jit(solution)/shard_map/ppermute | solution.py:196
  85.4 8.7 %collective-permute-start.9 = (bf16[16,4096]{1,0:T(8,128)(2,1)S(1)}, bf16[16,4096]{1,0:T(8,128)(2,1)S(1)}, u32[]{:S(2)}, u32[]{:S(2)}) collective-permute-start(bf16[16,4096]{1,0:T(8,128)(2,1)S(1)} %pad_maximum_fusion.2), channel_id=1, source_target_pairs={{0,32},{1,33},{2,34},{3,35},{4,36},{5,37},{6,38},{7,39},{8,40},{9,... | collective-permute-start | bytes 393224 | tf_op jit(solution)/shard_map/ppermute | solution.py:196
  87.5 0.9 copy-start.2
  88.6 0.7 copy-start.7
  89.3 0.7 copy-start.8
where the time goes:
time: 101 us
  starting transfers between devices  57.7 us (57%)
  waiting for transfers between devices  22.3 us (22%)
  Pallas kernels  12.7 us (13%)
  local copies, waits for them, and re-layouts  7.6 us (8%)
    ppermute x11, starting transfers between devices, send(): return lax.ppermute(x, axes, pairs)  57.7 us
    ppermute x11, waiting for transfers between devices, send(): return lax.ppermute(x, axes, pairs)  22.3 us
    pallas_call x2, Pallas kernels, section(): pl.pallas_call(functools.partial(section_kernel, size), out_shape=jax.Sha...  12.7 us
    unnamed x18, local copies, waits for them, and re-layouts  3.51 us
  transfers between devices with their start and end apart: 11, of which 8 were waited for; matrix products, arithmetic and copies ran while one was open for 2% of the time, Pallas kernels for 0%

commit v1 on v0

v1 whole, which is shorter than its diff:
```python
import functools

import jax
import jax.numpy as jnp
from jax import lax
from jax.experimental import pallas as pl
from jax.experimental.pallas import tpu as pltpu
from jax.sharding import PartitionSpec as P

ROWS = 64
COLS = 32
CH = 64
HALO = 16
TALL = ROWS + 2 * HALO
F32 = jnp.float32
BF16 = jnp.bfloat16


def lane_group(width, rows):
    return lax.broadcasted_iota(jnp.int32, (rows, 128), 1) // width


def build_weights(down, up, w1, w2, w3, w4):
    by32 = lane_group(32, 64)
    by64 = lane_group(64, 32)
    zero_down = jnp.zeros((64, 128), BF16)
    zero_up = jnp.zeros((32, 128), BF16)
    for p in range(3):
        for i in range(8):
            block = zero_down
            for q in range(3):
                o = i - 1 - q
                if 0 <= o < 4:
                    block = jnp.where(by32 == o, down[0, p, q], block)
            w1[i * 64 : (i + 1) * 64, p * 128 : (p + 1) * 128] = block
        for i in range(8):
            for half in range(2):
                block = zero_up
                for q in range(3):
                    o = i - 2 * q
                    if 0 <= o < 4 and o // 2 == half:
                        block = jnp.where(by64 == o % 2, up[0, p, q], block)
                w2[i * 32 : (i + 1) * 32, half * 384 + p * 128 : half * 384 + p * 128 + 128] = block
        for t in range(4):
            for e in range(2):
                block = zero_down
                for u in range(2):
                    q = t - u
                    if 0 <= q < 3:
                        block = jnp.where(by32 == 2 * u + e, down[1, p, q], block)
                w3[t * 128 + e * 64 : t * 128 + e * 64 + 64, p * 128 : (p + 1) * 128] = block
        for q in range(3):
            for g in range(4):
                for half in range(2):
                    block = zero_up
                    if g // 2 == half:
                        block = jnp.where(by64 == g % 2, up[1, p, q], block)
                    w4[
                        q * 128 + g * 32 : q * 128 + g * 32 + 32,
                        p * 256 + half * 128 : p * 256 + half * 128 + 128,
                    ] = block


def section_kernel(
    spots, bars, at, *refs
):
    pieces, refs = refs[: len(spots)], refs[len(spots) :]
    down, down_bias, up, up_bias, out, v, h1, h2, w1, w2, w3, w4 = refs
    build_weights(down, up, w1, w2, w3, w4)
    low_col, high_col, cut_low, cut_high = at[0], at[1], at[2], at[3]
    low_row, high_row = bars

    nothing = jnp.zeros((TALL, 128), BF16)
    v[0] = nothing
    v[33] = nothing
    h1[16] = nothing
    h2[12] = nothing
    for piece, (row, pair) in zip(pieces, spots):
        for i in range(piece.shape[1] // 128):
            v[pair + i + 1, row : row + piece.shape[0], :] = piece[:, i * 128 : (i + 1) * 128]

    sub = lax.broadcasted_iota(jnp.int32, (8, 128), 0)

    def cut(d):
        keep_top = jnp.where((sub >= 8 - d) & (cut_low > 0), 0.0, 1.0)
        keep_low = jnp.where((sub < d) & (cut_high > 0), 0.0, 1.0)
        return keep_top, keep_low

    def wide_dot(chunks, w, lo, hi):
        lhs = jnp.concatenate([jnp.concatenate(c, axis=0) for c in chunks], axis=1)
        return jnp.dot(lhs, w[:, lo:hi], preferred_element_type=F32)

    def parts(res, g, keep, lo, n):
        part = res[g * TALL : (g + 1) * TALL]
        top = part[:, lo : lo + 128]
        mid = part[:, n + lo : n + lo + 128]
        low = part[:, 2 * n + lo : 2 * n + lo + 128]
        top = jnp.concatenate(
            [top[: low_row - 8], top[low_row - 8 : low_row] * keep[0], top[low_row:]], axis=0
        )
        low = jnp.concatenate(
            [low[:high_row], low[high_row : high_row + 8] * keep[1], low[high_row + 8 :]], axis=0
        )
        return top, mid, low

    def taps(res, g, d, keep, lo, n):
        top, mid, low = parts(res, g, keep, lo, n)
        return pltpu.roll(top, d, 0) + mid + pltpu.roll(low, TALL - d, 0)

    def first_down(jj, _):
        j0 = jj * 4
        keep = cut(1)

        def pair_of(j, t):
            if t == 0:
                return jnp.where(j == 2 * low_col, 33, 2 * j)
            if t == 3:
                return jnp.where(j == 2 * high_col - 1, 33, 2 * j + 3)
            return 2 * j + t

        chunks = [[v[pair_of(j0 + g, t)] for g in range(4)] for t in range(4)]
        res = wide_dot(chunks, w1, 0, 384)
        for g in range(4):
            hidden = jnp.maximum(taps(res, g, 1, keep, 0, 128) + down_bias[0:1], 0.0)
            h1[j0 + g] = hidden.astype(BF16)
        return 0

    lax.fori_loop(0, 4, first_down, 0)

    def first_up(kk, _):
        k0 = kk * 3
        keep = cut(2)
        for half in range(2):
            hidden = []
            for g in range(3):
                k = k0 + g
                near, far = k, k + 1
                if half == 0:
                    far = jnp.where(far == 2 * high_col, 16, far)
                else:
                    near = jnp.where(far == 2 * low_col, 16, near)
                hidden.append((near, far))
            chunks = [[h1[pair[t]] for pair in hidden] for t in range(2)]
            res = wide_dot(chunks, w2, half * 384, half * 384 + 384)
            for g in range(3):
                i = 2 * (k0 + g) + 1 + half
                update = taps(res, g, 2, keep, 0, 128) + up_bias[0:1]
                v[i + 1] = (v[i + 1].astype(F32) + update).astype(BF16)
        return 0

    lax.fori_loop(0, 5, first_up, 0)

    def second_down(mm, _):
        groups = [(1 + 2 * mm + dm, s) for dm in range(2) for s in range(2)]
        keep = cut(4)

        def pair_of(m, s, t):
            if t == 0:
                return jnp.where(m == low_col, 33, 4 * m + s - 1)
            if t == 3:
                return jnp.where(m == high_col - 1, 33, 4 * m + s + 5)
            return 4 * m + s - 1 + 2 * t

        res = wide_dot([[v[pair_of(m, s, t)] for m, s in groups] for t in range(4)], w3, 0, 384)
        for g, (m, s) in enumerate(groups):
            hidden = jnp.maximum(taps(res, g, 4, keep, 0, 128) + down_bias[1:2], 0.0)
            h2[2 * (m - 1) + s] = hidden.astype(BF16)
        return 0

    lax.fori_loop(0, 3, second_down, 0)

    def second_up(mm, _):
        groups = [(2 + 2 * mm + dm, s) for dm in range(2) for s in range(2)]
        keep = cut(8)

        def group_of(m, s, q):
            if q == 0:
                return jnp.where(m == low_col, 12, 2 * (m - 2) + s)
            if q == 2:
                return jnp.where(m == high_col - 1, 12, 2 * m + s)
            return 2 * (m - 1) + s

        res = wide_dot([[h2[group_of(m, s, q)] for m, s in groups] for q in range(3)], w4, 0, 768)
        for g, (m, s) in enumerate(groups):
            for half in range(2):
                top, mid, low = parts(res, g, keep, half * 128, 256)
                update = top[8:72] + mid[16:80] + low[24:88] + up_bias[1:2]
                i = 4 * m + s + 2 * half
                value = v[i + 1][HALO : HALO + ROWS].astype(F32) + update
                at_lane = pl.multiple_of((i - 8) * 128, 128)
                out[:, pl.ds(at_lane, 128)] = value.astype(BF16)
        return 0

    lax.fori_loop(0, 2, second_up, 0)


def section(spots, bars, at, pieces, down, down_bias, up, up_bias):
    vmem = pl.BlockSpec(memory_space=pltpu.VMEM)
    return pl.pallas_call(
        functools.partial(section_kernel, spots, bars),
        out_shape=jax.ShapeDtypeStruct((ROWS, COLS * CH), BF16),
        in_specs=[pl.BlockSpec(memory_space=pltpu.SMEM)] + [vmem] * (len(spots) + 4),
        out_specs=vmem,
        scratch_shapes=[
            pltpu.VMEM((34, TALL, 128), BF16),
            pltpu.VMEM((17, TALL, 128), BF16),
            pltpu.VMEM((13, TALL, 128), BF16),
            pltpu.VMEM((512, 384), BF16),
            pltpu.VMEM((256, 768), BF16),
            pltpu.VMEM((512, 384), BF16),
            pltpu.VMEM((384, 768), BF16),
        ],
        compiler_params=pltpu.CompilerParams(vmem_limit_bytes=32 << 20),
    )(at, *pieces, down, down_bias, up, up_bias)


AHEAD = ((0, 0), (0, 16), (64, 0), (64, 16))
BEHIND = ((32, 16), (32, 0), (0, 16), (0, 0))


def solution(mesh):
    row_count, col_count = mesh.shape["row"], mesh.shape["col"]
    flip = row_count // 4
    axes = ("row", "col")

    def send(x, target):
        pairs = []
        for r in range(row_count):
            for c in range(col_count):
                row, col = target(r, c)
                to = (row % row_count) * col_count + col % col_count
                pairs.append((r * col_count + c, to))
        return lax.ppermute(x, axes, pairs)

    def with_ahead(x):
        corner = send(x[:32], lambda r, c: (r - 1, c - 1))
        right = send(x, lambda r, c: (r, c - 1))
        below = send(x[:32], lambda r, c: (r - 1, c))
        return x, right, below, corner

    def with_behind(x):
        corner = send(x[32:], lambda r, c: (r + 1, c + 1))
        left = send(x, lambda r, c: (r, c + 1))
        above = send(x[32:], lambda r, c: (r + 1, c))
        return x, left, above, corner

    def mirrored(x, parity):
        turned = x.reshape(2, 32, 32, CH).transpose(0, 2, 1, 3).reshape(2, 32, 32 * CH)
        near = lax.dynamic_index_in_dim(turned, parity, 0, keepdims=False)
        far = lax.dynamic_index_in_dim(turned, 1 - parity, 0, keepdims=False)
        far = send(far, lambda r, c: (r ^ flip, c))
        near = send(near, lambda r, c: (c // 2, 2 * r + c % 2))
        far = send(far, lambda r, c: (c // 2, 2 * (r ^ flip) + 1 - c % 2))
        even = jnp.concatenate([near, far], axis=0)
        odd = jnp.concatenate([far, near], axis=0)
        return jnp.where(parity == 0, even, odd)

    def per_device(contact, d1, db1, u1, ub1, d2, db2, u2, ub2):
        row, col = lax.axis_index("row"), lax.axis_index("col")
        first_row, last_row = row == 0, row == row_count - 1
        first_col, last_col = col == 0, col == col_count - 1

        def flags(low_at, low_col, high_at, high_col, low_row, high_row):
            return jnp.stack(
                [
                    jnp.where(low_col, low_at, -1),
                    jnp.where(high_col, high_at, -1),
                    low_row.astype(jnp.int32),
                    high_row.astype(jnp.int32),
                ]
            ).astype(jnp.int32)

        def prepared(down, down_bias, up, up_bias):
            return (
                jnp.tile(down.transpose(0, 1, 2, 4, 3), (1, 1, 1, 1, 4)),
                jnp.tile(down_bias, (1, 4)),
                jnp.tile(up.transpose(0, 1, 2, 4, 3), (1, 1, 1, 1, 2)),
                jnp.tile(up_bias, (1, 2)),
            )

        at = flags(4, last_col, 4, last_col, last_row, last_row)
        first = section(AHEAD, (64, 64), at, with_ahead(contact), *prepared(d1, db1, u1, ub1))
        flipped = mirrored(first, col % 2)
        symmetric = ((first.astype(F32) + flipped.astype(F32)) * 0.5).astype(BF16)
        at = flags(2, first_col, 6, last_col, first_row, last_row)
        return section(BEHIND, (16, 80), at, with_behind(symmetric), *prepared(d2, db2, u2, ub2))

    in_specs = (P("row", "col"), P(), P(), P(), P(), P(), P(), P(), P())
    return jax.shard_map(
        per_device, mesh=mesh, in_specs=in_specs, out_specs=P("row", "col"), check_vma=False
    )
```

time: 101 us -> 89.1 us (0.88)
  the two profiles are of different devices: /device:TPU:12 before, /device:TPU:1 now
where the time goes in v1:
time: 89.1 us; the launch traced here: 88.7 us
  starting transfers between devices  56.2 us (63%)
  Pallas kernels  13 us (15%)
  waiting for transfers between devices  11.5 us (13%)
  local copies, waits for them, and re-layouts  7.43 us (8%)
    ppermute x9, starting transfers between devices, send(): return lax.ppermute(x, axes, pairs)  56.2 us
    pallas_call x2, Pallas kernels, section(): pl.pallas_call(functools.partial(section_kernel, spots, bars), out_shape=...  13 us
    ppermute x9, waiting for transfers between devices, send(): return lax.ppermute(x, axes, pairs)  11.5 us
    unnamed x18, local copies, waits for them, and re-layouts  3.51 us
  transfers between devices with their start and end apart: 9, of which 4 were waited for; matrix products, arithmetic and copies ran while one was open for 3% of the time, Pallas kernels for 0%

profile of v1, /device:TPU:1, one launch (start us, length us, event | category | flops | bytes accessed | tf_op | source)
XLA Modules:
  0.0 88.7 jit_solution(14964970903977643115)
XLA Ops:
  0.0 13.1 %collective-permute-start = (bf16[64,2048]{1,0:T(8,128)(2,1)}, bf16[64,2048]{1,0:T(8,128)(2,1)S(1)}, u32[]{:S(2)}, u32[]{:S(2)}) collective-permute-start(bf16[64,2048]{1,0:T(8,128)(2,1)} %refs_0_.1), channel_id=1, source_target_pairs={{0,31},{1,0},{2,1},{3,2},{4,3},{5,4},{6,5},{7,6},{8,7},{9,8},{10,9... | collective-permute-start | bytes 786440 | tf_op jit(solution)/shard_map/ppermute | solution.py:233
  13.1 0.9 %slice.8 = bf16[32,2048]{1,0:T(8,128)(2,1)S(1)} slice(bf16[64,2048]{1,0:T(8,128)(2,1)} %refs_0_.1), slice={[0:32], [0:2048]} | slice | bytes 262144 | tf_op jit(solution)/shard_map/slice | solution.py:238
  14.0 2.9 %collective-permute-start.1 = (bf16[32,2048]{1,0:T(8,128)(2,1)S(1)}, bf16[32,2048]{1,0:T(8,128)(2,1)S(1)}, u32[]{:S(2)}, u32[]{:S(2)}) collective-permute-start(bf16[32,2048]{1,0:T(8,128)(2,1)S(1)} %slice.8), channel_id=1, source_target_pairs={{0,480},{1,481},{2,482},{3,483},{4,484},{5,485},{6,486},{7,487},{8... | collective-permute-start | bytes 393224 | tf_op jit(solution)/shard_map/ppermute | solution.py:233
  16.9 6.2 %collective-permute-start.2 = (bf16[32,2048]{1,0:T(8,128)(2,1)S(1)}, bf16[32,2048]{1,0:T(8,128)(2,1)S(1)}, u32[]{:S(2)}, u32[]{:S(2)}) collective-permute-start(bf16[32,2048]{1,0:T(8,128)(2,1)S(1)} %slice.8), channel_id=1, source_target_pairs={{0,511},{1,480},{2,481},{3,482},{4,483},{5,484},{6,485},{7,486},{8... | collective-permute-start | bytes 393224 | tf_op jit(solution)/shard_map/ppermute | solution.py:233
  23.2 0.3 copy.13.refs_4_
  23.5 0.6 copy-done.1
  24.1 0.2 tile.36
  24.4 0.2 tile.37.refs_6_
  24.5 0.5 copy-done.5
  25.1 0.6 copy-done.6
  25.9 0.4 collective-permute-done.2.refs_3_
  26.2 6.1 %shard_map.91 = bf16[64,2048]{1,0:T(8,128)(2,1)S(1)} custom-call(s32[4]{0:T(128)S(1)} %add_add_fusion.1.at, bf16[64,2048]{1,0:T(8,128)(2,1)S(1)} %copy-done, bf16[64,2048]{1,0:T(8,128)(2,1)S(1)} %collective-permute-done.refs_1_, bf16[32,2048]{1,0:T(8,128)(2,1)S(1)} %collective-permute-done.1.refs_2_, bf16[32,2048]{1,0:T(8,128)(2,1)S(1)} %collective-permute-done.2.refs_3_, ...), custom_call_target="tpu_custom_call" | custom-call | tf_op jit(solution)/shard_map/pallas_call | solution.py:199
  32.4 0.5 reshape.38
  32.9 0.2 copy.14
  33.1 0.5 reshape.39
  33.6 3.1 %collective-permute-start.4 = (bf16[32,2048]{1,0:T(8,128)(2,1)S(1)}, bf16[32,2048]{1,0:T(8,128)(2,1)S(1)}, u32[]{:S(2)}, u32[]{:S(2)}) collective-permute-start(bf16[32,2048]{1,0:T(8,128)(2,1)S(1)} %get-tuple-element.6), channel_id=1, source_target_pairs={{0,128},{1,129},{2,130},{3,131},{4,132},{5,133},{6,134},{7,135},{8... | collective-permute-start | bytes 393224 | tf_op jit(solution)/shard_map/ppermute | solution.py:233
  36.7 1.9 %collective-permute-start.3 = (bf16[32,2048]{1,0:T(8,128)(2,1)S(1)}, bf16[32,2048]{1,0:T(8,128)(2,1)S(1)}, u32[]{:S(2)}, u32[]{:S(2)}) collective-permute-start(bf16[32,2048]{1,0:T(8,128)(2,1)S(1)} %get-tuple-element.5), channel_id=1, source_target_pairs={{0,0},{1,1},{2,32},{3,33},{4,64},{5,65},{6,96},{7,97},{8,128},{9,1... | collective-permute-start | bytes 393224 | tf_op jit(solution)/shard_map/ppermute | solution.py:233
  38.7 0.8 collective-permute-done.4
  39.4 9.6 %collective-permute-start.5 = (bf16[32,2048]{1,0:T(8,128)(2,1)S(1)}, bf16[32,2048]{1,0:T(8,128)(2,1)S(1)}, u32[]{:S(2)}, u32[]{:S(2)}) collective-permute-start(bf16[32,2048]{1,0:T(8,128)(2,1)S(1)} %collective-permute-done.4), channel_id=1, source_target_pairs={{0,9},{1,8},{2,41},{3,40},{4,73},{5,72},{6,105},{7,104},{8,137},{9... | collective-permute-start | bytes 393224 | tf_op jit(solution)/shard_map/ppermute | solution.py:233
  49.0 6.4 %collective-permute-done.5 = bf16[32,2048]{1,0:T(8,128)(2,1)S(1)} collective-permute-done((bf16[32,2048]{1,0:T(8,128)(2,1)S(1)}, bf16[32,2048]{1,0:T(8,128)(2,1)S(1)}, u32[]{:S(2)}, u32[]{:S(2)}) %collective-permute-start.5) | collective-permute-done | bytes 131104 | tf_op jit(solution)/shard_map/ppermute | solution.py:233
  55.4 0.1 multiply_convert_fusion.refs_0_
  55.5 2.1 %collective-permute-start.6 = (bf16[64,2048]{1,0:T(8,128)(2,1)S(1)}, bf16[64,2048]{1,0:T(8,128)(2,1)S(1)}, u32[]{:S(2)}, u32[]{:S(2)}) collective-permute-start(bf16[64,2048]{1,0:T(8,128)(2,1)S(1)} %multiply_convert_fusion.refs_0_), channel_id=1, source_target_pairs={{0,1},{1,2},{2,3},{3,4},{4,5},{5,6},{6,7},{7,8},{8,9},{9,10},{10,1... | collective-permute-start | bytes 786440 | tf_op jit(solution)/shard_map/ppermute | solution.py:233
  57.6 15.5 %collective-permute-start.7 = (bf16[32,2048]{1,0:T(8,128)(2,1)S(1)}, bf16[32,2048]{1,0:T(8,128)(2,1)S(1)}, u32[]{:S(2)}, u32[]{:S(2)}) collective-permute-start(bf16[32,2048]{1,0:T(8,128)(2,1)S(1)} %slice.10), channel_id=1, source_target_pairs={{0,32},{1,33},{2,34},{3,35},{4,36},{5,37},{6,38},{7,39},{8,40},{9,... | collective-permute-start | bytes 393224 | tf_op jit(solution)/shard_map/ppermute | solution.py:233
  73.1 1.9 %collective-permute-start.8 = (bf16[32,2048]{1,0:T(8,128)(2,1)S(1)}, bf16[32,2048]{1,0:T(8,128)(2,1)S(1)}, u32[]{:S(2)}, u32[]{:S(2)}) collective-permute-start(bf16[32,2048]{1,0:T(8,128)(2,1)S(1)} %slice.10), channel_id=1, source_target_pairs={{0,33},{1,34},{2,35},{3,36},{4,37},{5,38},{6,39},{7,40},{8,41},{9,... | collective-permute-start | bytes 393224 | tf_op jit(solution)/shard_map/ppermute | solution.py:233
  75.2 0.3 copy.15.refs_4_
  75.4 0.6 copy-done.2
  76.1 0.2 tile.84
  76.3 0.2 tile.85.refs_6_
  76.5 0.5 copy-done.7
  77.1 0.6 copy-done.8
  77.8 4.0 %collective-permute-done.8.refs_3_ = bf16[32,2048]{1,0:T(8,128)(2,1)S(1)} collective-permute-done((bf16[32,2048]{1,0:T(8,128)(2,1)S(1)}, bf16[32,2048]{1,0:T(8,128)(2,1)S(1)}, u32[]{:S(2)}, u32[]{:S(2)}) %collective-permute-start.8) | collective-permute-done | bytes 131104 | tf_op jit(solution)/shard_map/ppermute | solution.py:233
  81.8 6.9 %shard_map.92 = bf16[64,2048]{1,0:T(8,128)(2,1)} custom-call(s32[4]{0:T(128)S(1)} %add_add_fusion.at, bf16[64,2048]{1,0:T(8,128)(2,1)S(1)} %multiply_convert_fusion.refs_0_, bf16[64,2048]{1,0:T(8,128)(2,1)S(1)} %collective-permute-done.6.refs_1_, bf16[32,2048]{1,0:T(8,128)(2,1)S(1)} %collective-permute-done.7.refs_2_, ...), custom_call_target="tpu_custom_call" | custom-call | tf_op jit(solution)/shard_map/pallas_call | solution.py:199
  (31 shorter events, 0.8 us)
Async XLA Ops:
  0.0 23.1 %copy-start.3 = (bf16[2,3,3,32,64]{4,3,2,1,0:T(8,128)(2,1)S(1)}, bf16[2,3,3,32,64]{4,3,2,1,0:T(8,128)(2,1)}, u32[]{:S(2)}) copy-start(bf16[2,3,3,32,64]{4,3,2,1,0:T(8,128)(2,1)} %param.10) | copy-start | bytes 221188
  0.0 26.2 %collective-permute-start = (bf16[64,2048]{1,0:T(8,128)(2,1)}, bf16[64,2048]{1,0:T(8,128)(2,1)S(1)}, u32[]{:S(2)}, u32[]{:S(2)}) collective-permute-start(bf16[64,2048]{1,0:T(8,128)(2,1)} %refs_0_.1), channel_id=1, source_target_pairs={{0,31},{1,0},{2,1},{3,2},{4,3},{5,4},{6,5},{7,6},{8,7},{9,8},{10,9... | collective-permute-start | bytes 786440 | tf_op jit(solution)/shard_map/ppermute | solution.py:233
  14.0 11.9 %collective-permute-start.1 = (bf16[32,2048]{1,0:T(8,128)(2,1)S(1)}, bf16[32,2048]{1,0:T(8,128)(2,1)S(1)}, u32[]{:S(2)}, u32[]{:S(2)}) collective-permute-start(bf16[32,2048]{1,0:T(8,128)(2,1)S(1)} %slice.8), channel_id=1, source_target_pairs={{0,480},{1,481},{2,482},{3,483},{4,484},{5,485},{6,486},{7,487},{8... | collective-permute-start | bytes 393224 | tf_op jit(solution)/shard_map/ppermute | solution.py:233
  16.9 9.4 %collective-permute-start.2 = (bf16[32,2048]{1,0:T(8,128)(2,1)S(1)}, bf16[32,2048]{1,0:T(8,128)(2,1)S(1)}, u32[]{:S(2)}, u32[]{:S(2)}) collective-permute-start(bf16[32,2048]{1,0:T(8,128)(2,1)S(1)} %slice.8), channel_id=1, source_target_pairs={{0,511},{1,480},{2,481},{3,482},{4,483},{5,484},{6,485},{7,486},{8... | collective-permute-start | bytes 393224 | tf_op jit(solution)/shard_map/ppermute | solution.py:233
  23.2 0.9 %copy-start.1 = (bf16[2,3,3,64,32]{3,4,2,1,0:T(8,128)(2,1)S(1)}, bf16[2,3,3,64,32]{3,4,2,1,0:T(8,128)(2,1)}, u32[]{:S(2)}) copy-start(bf16[2,3,3,64,32]{3,4,2,1,0:T(8,128)(2,1)} %param.12) | copy-start | bytes 221188
  24.3 0.7 copy-start.5
  24.4 1.9 %copy-start = (bf16[64,2048]{1,0:T(8,128)(2,1)S(1)}, bf16[64,2048]{1,0:T(8,128)(2,1)}, u32[]{:S(2)}) copy-start(bf16[64,2048]{1,0:T(8,128)(2,1)} %refs_0_.1) | copy-start | bytes 786436
  25.0 0.7 copy-start.6
  33.6 5.8 %collective-permute-start.4 = (bf16[32,2048]{1,0:T(8,128)(2,1)S(1)}, bf16[32,2048]{1,0:T(8,128)(2,1)S(1)}, u32[]{:S(2)}, u32[]{:S(2)}) collective-permute-start(bf16[32,2048]{1,0:T(8,128)(2,1)S(1)} %get-tuple-element.6), channel_id=1, source_target_pairs={{0,128},{1,129},{2,130},{3,131},{4,132},{5,133},{6,134},{7,135},{8... | collective-permute-start | bytes 393224 | tf_op jit(solution)/shard_map/ppermute | solution.py:233
  36.7 12.3 %collective-permute-start.3 = (bf16[32,2048]{1,0:T(8,128)(2,1)S(1)}, bf16[32,2048]{1,0:T(8,128)(2,1)S(1)}, u32[]{:S(2)}, u32[]{:S(2)}) collective-permute-start(bf16[32,2048]{1,0:T(8,128)(2,1)S(1)} %get-tuple-element.5), channel_id=1, source_target_pairs={{0,0},{1,1},{2,32},{3,33},{4,64},{5,65},{6,96},{7,97},{8,128},{9,1... | collective-permute-start | bytes 393224 | tf_op jit(solution)/shard_map/ppermute | solution.py:233
  39.4 16.0 %collective-permute-start.5 = (bf16[32,2048]{1,0:T(8,128)(2,1)S(1)}, bf16[32,2048]{1,0:T(8,128)(2,1)S(1)}, u32[]{:S(2)}, u32[]{:S(2)}) collective-permute-start(bf16[32,2048]{1,0:T(8,128)(2,1)S(1)} %collective-permute-done.4), channel_id=1, source_target_pairs={{0,9},{1,8},{2,41},{3,40},{4,73},{5,72},{6,105},{7,104},{8,137},{9... | collective-permute-start | bytes 393224 | tf_op jit(solution)/shard_map/ppermute | solution.py:233
  55.5 19.6 %copy-start.4 = (bf16[2,3,3,32,64]{4,3,2,1,0:T(8,128)(2,1)S(1)}, bf16[2,3,3,32,64]{4,3,2,1,0:T(8,128)(2,1)}, u32[]{:S(2)}) copy-start(bf16[2,3,3,32,64]{4,3,2,1,0:T(8,128)(2,1)} %param.14) | copy-start | bytes 221188
  55.5 26.3 %collective-permute-start.6 = (bf16[64,2048]{1,0:T(8,128)(2,1)S(1)}, bf16[64,2048]{1,0:T(8,128)(2,1)S(1)}, u32[]{:S(2)}, u32[]{:S(2)}) collective-permute-start(bf16[64,2048]{1,0:T(8,128)(2,1)S(1)} %multiply_convert_fusion.refs_0_), channel_id=1, source_target_pairs={{0,1},{1,2},{2,3},{3,4},{4,5},{5,6},{6,7},{7,8},{8,9},{9,10},{10,1... | collective-permute-start | bytes 786440 | tf_op jit(solution)/shard_map/ppermute | solution.py:233
  57.6 20.2 %collective-permute-start.7 = (bf16[32,2048]{1,0:T(8,128)(2,1)S(1)}, bf16[32,2048]{1,0:T(8,128)(2,1)S(1)}, u32[]{:S(2)}, u32[]{:S(2)}) collective-permute-start(bf16[32,2048]{1,0:T(8,128)(2,1)S(1)} %slice.10), channel_id=1, source_target_pairs={{0,32},{1,33},{2,34},{3,35},{4,36},{5,37},{6,38},{7,39},{8,40},{9,... | collective-permute-start | bytes 393224 | tf_op jit(solution)/shard_map/ppermute | solution.py:233
  73.1 8.7 %collective-permute-start.8 = (bf16[32,2048]{1,0:T(8,128)(2,1)S(1)}, bf16[32,2048]{1,0:T(8,128)(2,1)S(1)}, u32[]{:S(2)}, u32[]{:S(2)}) collective-permute-start(bf16[32,2048]{1,0:T(8,128)(2,1)S(1)} %slice.10), channel_id=1, source_target_pairs={{0,33},{1,34},{2,35},{3,36},{4,37},{5,38},{6,39},{7,40},{8,41},{9,... | collective-permute-start | bytes 393224 | tf_op jit(solution)/shard_map/ppermute | solution.py:233
  75.2 0.9 %copy-start.2 = (bf16[2,3,3,64,32]{3,4,2,1,0:T(8,128)(2,1)S(1)}, bf16[2,3,3,64,32]{3,4,2,1,0:T(8,128)(2,1)}, u32[]{:S(2)}) copy-start(bf16[2,3,3,64,32]{3,4,2,1,0:T(8,128)(2,1)} %param.16) | copy-start | bytes 221188
  76.3 0.7 copy-start.7
  77.0 0.7 copy-start.8

commit v2 on v1

--- a/solution.py
+++ b/solution.py
@@ -62,11 +62,12 @@
 
 
 def section_kernel(
-    spots, bars, at, *refs
+    spots, bars, turn, at, *refs
 ):
     pieces, refs = refs[: len(spots)], refs[len(spots) :]
-    down, down_bias, up, up_bias, out, v, h1, h2, w1, w2, w3, w4 = refs
-    build_weights(down, up, w1, w2, w3, w4)
+    w1, w2, w3, w4, down_bias, up_bias, out = refs[:7]
+    turning = turn and refs[7:10]
+    v, h1, h2 = refs[-3:]
     low_col, high_col, cut_low, cut_high = at[0], at[1], at[2], at[3]
     low_row, high_row = bars
 
@@ -188,30 +189,58 @@
                 i = 4 * m + s + 2 * half
                 value = v[i + 1][HALO : HALO + ROWS].astype(F32) + update
                 at_lane = pl.multiple_of((i - 8) * 128, 128)
-                out[:, pl.ds(at_lane, 128)] = value.astype(BF16)
+                value = value.astype(BF16)
+                out[:, pl.ds(at_lane, 128)] = value
+                if turn:
+                    value = value.astype(F32)
+                    strip = pl.multiple_of((i - 8) * 128, 128)
+                    turning[2][pl.ds(strip, 64), :] = value
+                    turning[2][pl.ds(strip + 64, 64), :] = pltpu.roll(value, 64, 1)
         return 0
 
     lax.fori_loop(0, 2, second_up, 0)
 
-
-def section(spots, bars, at, pieces, down, down_bias, up, up_bias):
+    if turn:
+        near, far, lines = turning
+        left_half = lax.broadcasted_iota(jnp.int32, (32, 128), 1) < 64
+        for target, base in ((near, at[4] * 32), (far, (1 - at[4]) * 32)):
+            for j in range(16):
+                even = lines[pl.ds(base + 2 * j, 32, stride=64), :]
+                odd = lines[pl.ds(base + 2 * j + 1, 32, stride=64), :]
+                both = jnp.where(left_half, even, pltpu.roll(odd, 64, 1))
+                target[:, j * 128 : (j + 1) * 128] = both.astype(BF16)
+
+
+def weights(down, up):
     vmem = pl.BlockSpec(memory_space=pltpu.VMEM)
+    shapes = [(512, 384), (256, 768), (512, 384), (384, 768)]
     return pl.pallas_call(
-        functools.partial(section_kernel, spots, bars),
-        out_shape=jax.ShapeDtypeStruct((ROWS, COLS * CH), BF16),
-        in_specs=[pl.BlockSpec(memory_space=pltpu.SMEM)] + [vmem] * (len(spots) + 4),
-        out_specs=vmem,
-        scratch_shapes=[
-            pltpu.VMEM((34, TALL, 128), BF16),
-            pltpu.VMEM((17, TALL, 128), BF16),
-            pltpu.VMEM((13, TALL, 128), BF16),
-            pltpu.VMEM((512, 384), BF16),
-            pltpu.VMEM((256, 768), BF16),
-            pltpu.VMEM((512, 384), BF16),
-            pltpu.VMEM((384, 768), BF16),
-        ],
+        build_weights,
+        out_shape=[jax.ShapeDtypeStruct(shape, BF16) for shape in shapes],
+        in_specs=[vmem, vmem],
+        out_specs=[vmem] * 4,
+    )(down, up)
+
+
+def section(spots, bars, turn, at, pieces, matrices, down_bias, up_bias):
+    vmem = pl.BlockSpec(memory_space=pltpu.VMEM)
+    out_shape = [jax.ShapeDtypeStruct((ROWS, COLS * CH), BF16)]
+    scratch = [
+        pltpu.VMEM((34, TALL, 128), BF16),
+        pltpu.VMEM((17, TALL, 128), BF16),
+        pltpu.VMEM((13, TALL, 128), BF16),
+    ]
+    if turn:
+        out_shape += [jax.ShapeDtypeStruct((32, 32 * CH), BF16)] * 2
+        scratch = [pltpu.VMEM((ROWS * COLS, 128), F32)] + scratch
+    return pl.pallas_call(
+        functools.partial(section_kernel, spots, bars, turn),
+        out_shape=out_shape,
+        in_specs=[pl.BlockSpec(memory_space=pltpu.SMEM)] + [vmem] * (len(spots) + 6),
+        out_specs=[vmem] * len(out_shape),
+        scratch_shapes=scratch,
         compiler_params=pltpu.CompilerParams(vmem_limit_bytes=32 << 20),
-    )(at, *pieces, down, down_bias, up, up_bias)
+    )(at, *pieces, *matrices, down_bias, up_bias)
 
 
 AHEAD = ((0, 0), (0, 16), (64, 0), (64, 16))
@@ -244,10 +273,7 @@
         above = send(x[32:], lambda r, c: (r + 1, c))
         return x, left, above, corner
 
-    def mirrored(x, parity):
-        turned = x.reshape(2, 32, 32, CH).transpose(0, 2, 1, 3).reshape(2, 32, 32 * CH)
-        near = lax.dynamic_index_in_dim(turned, parity, 0, keepdims=False)
-        far = lax.dynamic_index_in_dim(turned, 1 - parity, 0, keepdims=False)
+    def mirrored(near, far, parity):
         far = send(far, lambda r, c: (r ^ flip, c))
         near = send(near, lambda r, c: (c // 2, 2 * r + c % 2))
         far = send(far, lambda r, c: (c // 2, 2 * (r ^ flip) + 1 - c % 2))
@@ -267,23 +293,32 @@
                     jnp.where(high_col, high_at, -1),
                     low_row.astype(jnp.int32),
                     high_row.astype(jnp.int32),
+                    col % 2,
                 ]
             ).astype(jnp.int32)
 
-        def prepared(down, down_bias, up, up_bias):
-            return (
+        def matrices(down, up):
+            return weights(
                 jnp.tile(down.transpose(0, 1, 2, 4, 3), (1, 1, 1, 1, 4)),
-                jnp.tile(down_bias, (1, 4)),
                 jnp.tile(up.transpose(0, 1, 2, 4, 3), (1, 1, 1, 1, 2)),
-                jnp.tile(up_bias, (1, 2)),
             )
 
+        def biases(down_bias, up_bias):
+            return jnp.tile(down_bias, (1, 4)), jnp.tile(up_bias, (1, 2))
+
         at = flags(4, last_col, 4, last_col, last_row, last_row)
-        first = section(AHEAD, (64, 64), at, with_ahead(contact), *prepared(d1, db1, u1, ub1))
-        flipped = mirrored(first, col % 2)
+        pieces = with_ahead(contact)
+        first, near, far = section(
+            AHEAD, (64, 64), True, at, pieces, matrices(d1, u1), *biases(db1, ub1)
+        )
+        later = matrices(d2, u2)
+        flipped = mirrored(near, far, col % 2)
         symmetric = ((first.astype(F32) + flipped.astype(F32)) * 0.5).astype(BF16)
+        symmetric, later = lax.optimization_barrier((symmetric, later))
         at = flags(2, first_col, 6, last_col, first_row, last_row)
-        return section(BEHIND, (16, 80), at, with_behind(symmetric), *prepared(d2, db2, u2, ub2))
+        return section(
+            BEHIND, (16, 80), False, at, with_behind(symmetric), later, *biases(db2, ub2)
+        )[0]
 
     in_specs = (P("row", "col"), P(), P(), P(), P(), P(), P(), P(), P())
     return jax.shard_map(

time: 89.1 us -> 96.3 us (1.081)
  the two profiles are of different devices: /device:TPU:1 before, /device:TPU:8 now
where the time goes in v2:
time: 96.3 us; the launch traced here: 95.6 us
  starting transfers between devices  56.5 us (59%)
  Pallas kernels  17.9 us (19%)
  local copies, waits for them, and re-layouts  13 us (13%)
  waiting for transfers between devices  7.82 us (8%)
    ppermute x9, starting transfers between devices, send(): return lax.ppermute(x, axes, pairs)  56.5 us
    pallas_call x2, Pallas kernels, section(): pl.pallas_call(functools.partial(section_kernel, spots, bars, turn), out_...  13.2 us
    ppermute x9, waiting for transfers between devices, send(): return lax.ppermute(x, axes, pairs)  7.82 us
    unnamed x34, local copies, waits for them, and re-layouts  7.34 us
    pallas_call x2, Pallas kernels, weights(): pl.pallas_call(build_weights, out_shape=[jax.ShapeDtypeStruct(shape, BF16...  4.74 us
    another operation x4, local copies, waits for them, and re-layouts, matrices(): jnp.tile(up.transpose(0, 1, 2, 4, 3), (1, 1, 1, 1, 2))  2.1 us
    another operation x4, local copies, waits for them, and re-layouts, matrices(): jnp.tile(down.transpose(0, 1, 2, 4, 3), (1, 1, 1, 1, 4))  2.07 us
  transfers between devices with their start and end apart: 9, of which 3 were waited for; matrix products, arithmetic and copies ran while one was open for 6% of the time, Pallas kernels for 5%

profile of v2, /device:TPU:8, one launch (start us, length us, event | category | flops | bytes accessed | tf_op | source)
XLA Modules:
  0.0 95.6 jit_solution(218556018212801677)
XLA Ops:
  0.0 11.4 %collective-permute-start = (bf16[64,2048]{1,0:T(8,128)(2,1)}, bf16[64,2048]{1,0:T(8,128)(2,1)S(1)}, u32[]{:S(2)}, u32[]{:S(2)}) collective-permute-start(bf16[64,2048]{1,0:T(8,128)(2,1)} %refs_0_.1), channel_id=1, source_target_pairs={{0,31},{1,0},{2,1},{3,2},{4,3},{5,4},{6,5},{7,6},{8,7},{9,8},{10,9... | collective-permute-start | bytes 786440 | tf_op jit(solution)/shard_map/ppermute | solution.py:262
  11.4 0.9 slice.8
  12.3 5.9 %collective-permute-start.1 = (bf16[32,2048]{1,0:T(8,128)(2,1)S(1)}, bf16[32,2048]{1,0:T(8,128)(2,1)S(1)}, u32[]{:S(2)}, u32[]{:S(2)}) collective-permute-start(bf16[32,2048]{1,0:T(8,128)(2,1)S(1)} %slice.8), channel_id=1, source_target_pairs={{0,480},{1,481},{2,482},{3,483},{4,484},{5,485},{6,486},{7,487},{8... | collective-permute-start | bytes 393224 | tf_op jit(solution)/shard_map/ppermute | solution.py:262
  18.2 2.4 %collective-permute-start.2 = (bf16[32,2048]{1,0:T(8,128)(2,1)S(1)}, bf16[32,2048]{1,0:T(8,128)(2,1)S(1)}, u32[]{:S(2)}, u32[]{:S(2)}) collective-permute-start(bf16[32,2048]{1,0:T(8,128)(2,1)S(1)} %slice.8), channel_id=1, source_target_pairs={{0,511},{1,480},{2,481},{3,482},{4,483},{5,484},{6,485},{7,486},{8... | collective-permute-start | bytes 393224 | tf_op jit(solution)/shard_map/ppermute | solution.py:262
  20.8 0.9 copy.12.down
  21.7 0.2 tile.34
  22.0 0.8 tile.35.up
  23.0 2.4 %shard_map.91 = (bf16[512,384]{1,0:T(8,128)(2,1)}, bf16[256,768]{1,0:T(8,128)(2,1)}, bf16[512,384]{1,0:T(8,128)(2,1)}, bf16[384,768]{1,0:T(8,128)(2,1)}) custom-call(bf16[2,3,3,64,128]{4,3,2,1,0:T(8,128)(2,1)} %copy.12.down, bf16[2,3,3,32,128]{4,3,2,1,0:T(8,128)(2,1)} %tile.35.up), custom_call_target="tpu_custom_call" | custom-call | tf_op jit(solution)/shard_map/pallas_call | solution.py:217
  25.5 1.1 %copy-done.2 = bf16[384,768]{1,0:T(8,128)(2,1)S(1)} copy-done((bf16[384,768]{1,0:T(8,128)(2,1)S(1)}, bf16[384,768]{1,0:T(8,128)(2,1)}, u32[]{:S(2)}) %copy-start.2) | copy-done | bytes 589848
  26.5 1.0 %copy-done.3 = bf16[512,384]{1,0:T(8,128)(2,1)S(1)} copy-done((bf16[512,384]{1,0:T(8,128)(2,1)S(1)}, bf16[512,384]{1,0:T(8,128)(2,1)}, u32[]{:S(2)}) %copy-start.3) | copy-done | bytes 393240
  27.5 1.0 %copy-done.4 = bf16[256,768]{1,0:T(8,128)(2,1)S(1)} copy-done((bf16[256,768]{1,0:T(8,128)(2,1)S(1)}, bf16[256,768]{1,0:T(8,128)(2,1)}, u32[]{:S(2)}) %copy-start.4) | copy-done | bytes 393240
  28.5 1.0 %copy-done.5 = bf16[512,384]{1,0:T(8,128)(2,1)S(1)} copy-done((bf16[512,384]{1,0:T(8,128)(2,1)S(1)}, bf16[512,384]{1,0:T(8,128)(2,1)}, u32[]{:S(2)}) %copy-start.5) | copy-done | bytes 393240
  29.5 6.6 %shard_map.92 = (bf16[64,2048]{1,0:T(8,128)(2,1)S(1)}, bf16[32,2048]{1,0:T(8,128)(2,1)S(1)}, bf16[32,2048]{1,0:T(8,128)(2,1)S(1)}) custom-call(s32[5]{0:T(128)S(1)} %stack.43.at, bf16[64,2048]{1,0:T(8,128)(2,1)S(1)} %copy-done, bf16[64,2048]{1,0:T(8,128)(2,1)S(1)} %collective-permute-done.refs_1_, bf16[32,2048]{1,0:T(8,128)(2,1)S(1)} %collective-permute-done.1.refs_2_, ...), custom_call_target="tpu_custom_call" | custom-call | tf_op jit(solution)/shard_map/pallas_call | solution.py:236
  36.1 1.9 %collective-permute-start.4 = (bf16[32,2048]{1,0:T(8,128)(2,1)S(1)}, bf16[32,2048]{1,0:T(8,128)(2,1)S(1)}, u32[]{:S(2)}, u32[]{:S(2)}) collective-permute-start(bf16[32,2048]{1,0:T(8,128)(2,1)S(1)} %get-tuple-element.27), channel_id=1, source_target_pairs={{0,128},{1,129},{2,130},{3,131},{4,132},{5,133},{6,134},{7,135},{8... | collective-permute-start | bytes 393224 | tf_op jit(solution)/shard_map/ppermute | solution.py:262
  38.0 5.5 %collective-permute-start.3 = (bf16[32,2048]{1,0:T(8,128)(2,1)S(1)}, bf16[32,2048]{1,0:T(8,128)(2,1)S(1)}, u32[]{:S(2)}, u32[]{:S(2)}) collective-permute-start(bf16[32,2048]{1,0:T(8,128)(2,1)S(1)} %get-tuple-element.26), channel_id=1, source_target_pairs={{0,0},{1,1},{2,32},{3,33},{4,64},{5,65},{6,96},{7,97},{8,128},{9,1... | collective-permute-start | bytes 393224 | tf_op jit(solution)/shard_map/ppermute | solution.py:262
  43.6 0.5 collective-permute-done.4
  44.1 12.8 %collective-permute-start.5 = (bf16[32,2048]{1,0:T(8,128)(2,1)S(1)}, bf16[32,2048]{1,0:T(8,128)(2,1)S(1)}, u32[]{:S(2)}, u32[]{:S(2)}) collective-permute-start(bf16[32,2048]{1,0:T(8,128)(2,1)S(1)} %collective-permute-done.4), channel_id=1, source_target_pairs={{0,9},{1,8},{2,41},{3,40},{4,73},{5,72},{6,105},{7,104},{8,137},{9... | collective-permute-start | bytes 393224 | tf_op jit(solution)/shard_map/ppermute | solution.py:262
  57.1 0.9 copy.13.down
  58.0 0.2 tile.82
  58.3 0.8 tile.83.up
  59.1 2.4 %shard_map.93 = (bf16[512,384]{1,0:T(8,128)(2,1)}, bf16[256,768]{1,0:T(8,128)(2,1)}, bf16[512,384]{1,0:T(8,128)(2,1)}, bf16[384,768]{1,0:T(8,128)(2,1)}) custom-call(bf16[2,3,3,64,128]{4,3,2,1,0:T(8,128)(2,1)} %copy.13.down, bf16[2,3,3,32,128]{4,3,2,1,0:T(8,128)(2,1)} %tile.83.up), custom_call_target="tpu_custom_call" | custom-call | tf_op jit(solution)/shard_map/pallas_call | solution.py:217
  61.5 0.5 collective-permute-done.5
  61.9 0.1 multiply_convert_fusion.refs_0_
  62.0 2.1 %collective-permute-start.6 = (bf16[64,2048]{1,0:T(8,128)(2,1)S(1)}, bf16[64,2048]{1,0:T(8,128)(2,1)S(1)}, u32[]{:S(2)}, u32[]{:S(2)}) collective-permute-start(bf16[64,2048]{1,0:T(8,128)(2,1)S(1)} %multiply_convert_fusion.refs_0_), channel_id=1, source_target_pairs={{0,1},{1,2},{2,3},{3,4},{4,5},{5,6},{6,7},{7,8},{8,9},{9,10},{10,1... | collective-permute-start | bytes 786440 | tf_op jit(solution)/shard_map/ppermute | solution.py:262
  64.1 5.0 %collective-permute-start.7 = (bf16[32,2048]{1,0:T(8,128)(2,1)S(1)}, bf16[32,2048]{1,0:T(8,128)(2,1)S(1)}, u32[]{:S(2)}, u32[]{:S(2)}) collective-permute-start(bf16[32,2048]{1,0:T(8,128)(2,1)S(1)} %slice.9), channel_id=1, source_target_pairs={{0,32},{1,33},{2,34},{3,35},{4,36},{5,37},{6,38},{7,39},{8,40},{9,... | collective-permute-start | bytes 393224 | tf_op jit(solution)/shard_map/ppermute | solution.py:262
  69.2 9.5 %collective-permute-start.8 = (bf16[32,2048]{1,0:T(8,128)(2,1)S(1)}, bf16[32,2048]{1,0:T(8,128)(2,1)S(1)}, u32[]{:S(2)}, u32[]{:S(2)}) collective-permute-start(bf16[32,2048]{1,0:T(8,128)(2,1)S(1)} %slice.9), channel_id=1, source_target_pairs={{0,33},{1,34},{2,35},{3,36},{4,37},{5,38},{6,39},{7,40},{8,41},{9,... | collective-permute-start | bytes 393224 | tf_op jit(solution)/shard_map/ppermute | solution.py:262
  78.7 0.7 copy-done.15
  79.4 0.6 copy-done.16
  80.2 6.8 %collective-permute-done.8.refs_3_ = bf16[32,2048]{1,0:T(8,128)(2,1)S(1)} collective-permute-done((bf16[32,2048]{1,0:T(8,128)(2,1)S(1)}, bf16[32,2048]{1,0:T(8,128)(2,1)S(1)}, u32[]{:S(2)}, u32[]{:S(2)}) %collective-permute-start.8) | collective-permute-done | bytes 131104 | tf_op jit(solution)/shard_map/ppermute | solution.py:262
  87.0 1.0 %copy-done.7 = bf16[256,768]{1,0:T(8,128)(2,1)S(1)} copy-done((bf16[256,768]{1,0:T(8,128)(2,1)S(1)}, bf16[256,768]{1,0:T(8,128)(2,1)}, u32[]{:S(2)}) %copy-start.7) | copy-done | bytes 393240
  88.0 1.0 %copy-done.8 = bf16[512,384]{1,0:T(8,128)(2,1)S(1)} copy-done((bf16[512,384]{1,0:T(8,128)(2,1)S(1)}, bf16[512,384]{1,0:T(8,128)(2,1)}, u32[]{:S(2)}) %copy-start.8) | copy-done | bytes 393240
  89.0 6.6 %shard_map.94 = bf16[64,2048]{1,0:T(8,128)(2,1)} custom-call(s32[5]{0:T(128)S(1)} %stack.41.at, bf16[64,2048]{1,0:T(8,128)(2,1)S(1)} %multiply_convert_fusion.refs_0_, bf16[64,2048]{1,0:T(8,128)(2,1)S(1)} %collective-permute-done.6.refs_1_, bf16[32,2048]{1,0:T(8,128)(2,1)S(1)} %collective-permute-done.7.refs_2_, ...), custom_call_target="tpu_custom_call" | custom-call | tf_op jit(solution)/shard_map/pallas_call | solution.py:236
  (45 shorter events, 0.8 us)
Async XLA Ops:
  0.0 20.6 %copy-start.11 = (bf16[2,3,3,32,64]{4,3,2,1,0:T(8,128)(2,1)S(1)}, bf16[2,3,3,32,64]{4,3,2,1,0:T(8,128)(2,1)}, u32[]{:S(2)}) copy-start(bf16[2,3,3,32,64]{4,3,2,1,0:T(8,128)(2,1)} %param.10) | copy-start | bytes 221188
  0.0 25.4 %collective-permute-start = (bf16[64,2048]{1,0:T(8,128)(2,1)}, bf16[64,2048]{1,0:T(8,128)(2,1)S(1)}, u32[]{:S(2)}, u32[]{:S(2)}) collective-permute-start(bf16[64,2048]{1,0:T(8,128)(2,1)} %refs_0_.1), channel_id=1, source_target_pairs={{0,31},{1,0},{2,1},{3,2},{4,3},{5,4},{6,5},{7,6},{8,7},{9,8},{10,9... | collective-permute-start | bytes 786440 | tf_op jit(solution)/shard_map/ppermute | solution.py:262
  12.3 13.1 %collective-permute-start.1 = (bf16[32,2048]{1,0:T(8,128)(2,1)S(1)}, bf16[32,2048]{1,0:T(8,128)(2,1)S(1)}, u32[]{:S(2)}, u32[]{:S(2)}) collective-permute-start(bf16[32,2048]{1,0:T(8,128)(2,1)S(1)} %slice.8), channel_id=1, source_target_pairs={{0,480},{1,481},{2,482},{3,483},{4,484},{5,485},{6,486},{7,487},{8... | collective-permute-start | bytes 393224 | tf_op jit(solution)/shard_map/ppermute | solution.py:262
  18.2 7.2 %collective-permute-start.2 = (bf16[32,2048]{1,0:T(8,128)(2,1)S(1)}, bf16[32,2048]{1,0:T(8,128)(2,1)S(1)}, u32[]{:S(2)}, u32[]{:S(2)}) collective-permute-start(bf16[32,2048]{1,0:T(8,128)(2,1)S(1)} %slice.8), channel_id=1, source_target_pairs={{0,511},{1,480},{2,481},{3,482},{4,483},{5,484},{6,485},{7,486},{8... | collective-permute-start | bytes 393224 | tf_op jit(solution)/shard_map/ppermute | solution.py:262
  20.7 1.0 %copy-start.9 = (bf16[2,3,3,64,32]{3,4,2,1,0:T(8,128)(2,1)S(1)}, bf16[2,3,3,64,32]{3,4,2,1,0:T(8,128)(2,1)}, u32[]{:S(2)}) copy-start(bf16[2,3,3,64,32]{3,4,2,1,0:T(8,128)(2,1)} %param.12) | copy-start | bytes 221188
  21.9 0.9 copy-start.13
  22.0 0.9 copy-start.14
  22.8 2.7 %copy-start = (bf16[64,2048]{1,0:T(8,128)(2,1)S(1)}, bf16[64,2048]{1,0:T(8,128)(2,1)}, u32[]{:S(2)}) copy-start(bf16[64,2048]{1,0:T(8,128)(2,1)} %refs_0_.1) | copy-start | bytes 786436
  25.5 1.1 %copy-start.2 = (bf16[384,768]{1,0:T(8,128)(2,1)S(1)}, bf16[384,768]{1,0:T(8,128)(2,1)}, u32[]{:S(2)}) copy-start(bf16[384,768]{1,0:T(8,128)(2,1)} %get-tuple-element.24.refs_7_) | copy-start | bytes 1769476
  26.5 1.0 %copy-start.3 = (bf16[512,384]{1,0:T(8,128)(2,1)S(1)}, bf16[512,384]{1,0:T(8,128)(2,1)}, u32[]{:S(2)}) copy-start(bf16[512,384]{1,0:T(8,128)(2,1)} %get-tuple-element.21.refs_4_) | copy-start | bytes 1179652
  27.5 1.0 %copy-start.4 = (bf16[256,768]{1,0:T(8,128)(2,1)S(1)}, bf16[256,768]{1,0:T(8,128)(2,1)}, u32[]{:S(2)}) copy-start(bf16[256,768]{1,0:T(8,128)(2,1)} %get-tuple-element.22.refs_5_) | copy-start | bytes 1179652
  28.5 1.0 %copy-start.5 = (bf16[512,384]{1,0:T(8,128)(2,1)S(1)}, bf16[512,384]{1,0:T(8,128)(2,1)}, u32[]{:S(2)}) copy-start(bf16[512,384]{1,0:T(8,128)(2,1)} %get-tuple-element.23.refs_6_) | copy-start | bytes 1179652
  29.5 27.5 %copy-start.12 = (bf16[2,3,3,32,64]{4,3,2,1,0:T(8,128)(2,1)S(1)}, bf16[2,3,3,32,64]{4,3,2,1,0:T(8,128)(2,1)}, u32[]{:S(2)}) copy-start(bf16[2,3,3,32,64]{4,3,2,1,0:T(8,128)(2,1)} %param.14) | copy-start | bytes 221188
  36.1 8.0 %collective-permute-start.4 = (bf16[32,2048]{1,0:T(8,128)(2,1)S(1)}, bf16[32,2048]{1,0:T(8,128)(2,1)S(1)}, u32[]{:S(2)}, u32[]{:S(2)}) collective-permute-start(bf16[32,2048]{1,0:T(8,128)(2,1)S(1)} %get-tuple-element.27), channel_id=1, source_target_pairs={{0,128},{1,129},{2,130},{3,131},{4,132},{5,133},{6,134},{7,135},{8... | collective-permute-start | bytes 393224 | tf_op jit(solution)/shard_map/ppermute | solution.py:262
  38.0 23.4 %collective-permute-start.3 = (bf16[32,2048]{1,0:T(8,128)(2,1)S(1)}, bf16[32,2048]{1,0:T(8,128)(2,1)S(1)}, u32[]{:S(2)}, u32[]{:S(2)}) collective-permute-start(bf16[32,2048]{1,0:T(8,128)(2,1)S(1)} %get-tuple-element.26), channel_id=1, source_target_pairs={{0,0},{1,1},{2,32},{3,33},{4,64},{5,65},{6,96},{7,97},{8,128},{9,1... | collective-permute-start | bytes 393224 | tf_op jit(solution)/shard_map/ppermute | solution.py:262
  44.1 17.8 %collective-permute-start.5 = (bf16[32,2048]{1,0:T(8,128)(2,1)S(1)}, bf16[32,2048]{1,0:T(8,128)(2,1)S(1)}, u32[]{:S(2)}, u32[]{:S(2)}) collective-permute-start(bf16[32,2048]{1,0:T(8,128)(2,1)S(1)} %collective-permute-done.4), channel_id=1, source_target_pairs={{0,9},{1,8},{2,41},{3,40},{4,73},{5,72},{6,105},{7,104},{8,137},{9... | collective-permute-start | bytes 393224 | tf_op jit(solution)/shard_map/ppermute | solution.py:262
  57.1 1.0 %copy-start.10 = (bf16[2,3,3,64,32]{3,4,2,1,0:T(8,128)(2,1)S(1)}, bf16[2,3,3,64,32]{3,4,2,1,0:T(8,128)(2,1)}, u32[]{:S(2)}) copy-start(bf16[2,3,3,64,32]{3,4,2,1,0:T(8,128)(2,1)} %param.16) | copy-start | bytes 221188
  61.4 25.5 %copy-start.1 = (bf16[384,768]{1,0:T(8,128)(2,1)S(1)}, bf16[384,768]{1,0:T(8,128)(2,1)}, u32[]{:S(2)}) copy-start(bf16[384,768]{1,0:T(8,128)(2,1)} %get-tuple-element.36.refs_7_) | copy-start | bytes 1769476
  61.9 25.0 %copy-start.6 = (bf16[512,384]{1,0:T(8,128)(2,1)S(1)}, bf16[512,384]{1,0:T(8,128)(2,1)}, u32[]{:S(2)}) copy-start(bf16[512,384]{1,0:T(8,128)(2,1)} %get-tuple-element.33.refs_4_) | copy-start | bytes 1179652
  62.0 24.9 %collective-permute-start.6 = (bf16[64,2048]{1,0:T(8,128)(2,1)S(1)}, bf16[64,2048]{1,0:T(8,128)(2,1)S(1)}, u32[]{:S(2)}, u32[]{:S(2)}) collective-permute-start(bf16[64,2048]{1,0:T(8,128)(2,1)S(1)} %multiply_convert_fusion.refs_0_), channel_id=1, source_target_pairs={{0,1},{1,2},{2,3},{3,4},{4,5},{5,6},{6,7},{7,8},{8,9},{9,10},{10,1... | collective-permute-start | bytes 786440 | tf_op jit(solution)/shard_map/ppermute | solution.py:262
  64.1 16.1 %collective-permute-start.7 = (bf16[32,2048]{1,0:T(8,128)(2,1)S(1)}, bf16[32,2048]{1,0:T(8,128)(2,1)S(1)}, u32[]{:S(2)}, u32[]{:S(2)}) collective-permute-start(bf16[32,2048]{1,0:T(8,128)(2,1)S(1)} %slice.9), channel_id=1, source_target_pairs={{0,32},{1,33},{2,34},{3,35},{4,36},{5,37},{6,38},{7,39},{8,40},{9,... | collective-permute-start | bytes 393224 | tf_op jit(solution)/shard_map/ppermute | solution.py:262
  69.2 17.8 %collective-permute-start.8 = (bf16[32,2048]{1,0:T(8,128)(2,1)S(1)}, bf16[32,2048]{1,0:T(8,128)(2,1)S(1)}, u32[]{:S(2)}, u32[]{:S(2)}) collective-permute-start(bf16[32,2048]{1,0:T(8,128)(2,1)S(1)} %slice.9), channel_id=1, source_target_pairs={{0,33},{1,34},{2,35},{3,36},{4,37},{5,38},{6,39},{7,40},{8,41},{9,... | collective-permute-start | bytes 393224 | tf_op jit(solution)/shard_map/ppermute | solution.py:262
  78.7 0.7 copy-start.15
  79.4 0.7 copy-start.16
  87.0 1.0 %copy-start.7 = (bf16[256,768]{1,0:T(8,128)(2,1)S(1)}, bf16[256,768]{1,0:T(8,128)(2,1)}, u32[]{:S(2)}) copy-start(bf16[256,768]{1,0:T(8,128)(2,1)} %get-tuple-element.34.refs_5_) | copy-start | bytes 1179652
  88.0 1.0 %copy-start.8 = (bf16[512,384]{1,0:T(8,128)(2,1)S(1)}, bf16[512,384]{1,0:T(8,128)(2,1)}, u32[]{:S(2)}) copy-start(bf16[512,384]{1,0:T(8,128)(2,1)} %get-tuple-element.35.refs_6_) | copy-start | bytes 1179652

commit v3 on v2

--- a/solution.py
+++ b/solution.py
@@ -219,6 +219,7 @@
         out_shape=[jax.ShapeDtypeStruct(shape, BF16) for shape in shapes],
         in_specs=[vmem, vmem],
         out_specs=[vmem] * 4,
+        compiler_params=pltpu.CompilerParams(vmem_limit_bytes=8 << 20),
     )(down, up)
 
 
@@ -239,7 +240,7 @@
         in_specs=[pl.BlockSpec(memory_space=pltpu.SMEM)] + [vmem] * (len(spots) + 6),
         out_specs=[vmem] * len(out_shape),
         scratch_shapes=scratch,
-        compiler_params=pltpu.CompilerParams(vmem_limit_bytes=32 << 20),
+        compiler_params=pltpu.CompilerParams(vmem_limit_bytes=16 << 20),
     )(at, *pieces, *matrices, down_bias, up_bias)
 
 

time: 96.3 us -> 88 us (0.914)
  the two profiles are of different devices: /device:TPU:8 before, /device:TPU:1 now
where the time goes in v3:
time: 88 us; the launch traced here: 87.5 us
  starting transfers between devices  56.2 us (64%)
  Pallas kernels  13.7 us (16%)
  waiting for transfers between devices  11.3 us (13%)
  local copies, waits for them, and re-layouts  5.98 us (7%)
    ppermute x9, starting transfers between devices, send(): return lax.ppermute(x, axes, pairs)  56.2 us
    pallas_call x2, Pallas kernels, section(): pl.pallas_call(functools.partial(section_kernel, spots, bars, turn), out_...  13.2 us
    ppermute x9, waiting for transfers between devices, send(): return lax.ppermute(x, axes, pairs)  11.3 us
    unnamed x18, local copies, waits for them, and re-layouts  3.07 us
  transfers between devices with their start and end apart: 9, of which 4 were waited for; matrix products, arithmetic and copies ran while one was open for 3% of the time, Pallas kernels for 1%

profile of v3, /device:TPU:1, one launch (start us, length us, event | category | flops | bytes accessed | tf_op | source)
XLA Modules:
  0.0 87.5 jit_solution(8184536048759397461)
XLA Ops:
  0.0 13.1 %collective-permute-start = (bf16[64,2048]{1,0:T(8,128)(2,1)}, bf16[64,2048]{1,0:T(8,128)(2,1)S(1)}, u32[]{:S(2)}, u32[]{:S(2)}) collective-permute-start(bf16[64,2048]{1,0:T(8,128)(2,1)} %refs_0_.1), channel_id=1, source_target_pairs={{0,31},{1,0},{2,1},{3,2},{4,3},{5,4},{6,5},{7,6},{8,7},{9,8},{10,9... | collective-permute-start | bytes 786440 | tf_op jit(solution)/shard_map/ppermute | solution.py:263
  13.1 0.9 %slice.8 = bf16[32,2048]{1,0:T(8,128)(2,1)S(1)} slice(bf16[64,2048]{1,0:T(8,128)(2,1)} %refs_0_.1), slice={[0:32], [0:2048]} | slice | bytes 262144 | tf_op jit(solution)/shard_map/slice | solution.py:268
  14.0 2.9 %collective-permute-start.1 = (bf16[32,2048]{1,0:T(8,128)(2,1)S(1)}, bf16[32,2048]{1,0:T(8,128)(2,1)S(1)}, u32[]{:S(2)}, u32[]{:S(2)}) collective-permute-start(bf16[32,2048]{1,0:T(8,128)(2,1)S(1)} %slice.8), channel_id=1, source_target_pairs={{0,480},{1,481},{2,482},{3,483},{4,484},{5,485},{6,486},{7,487},{8... | collective-permute-start | bytes 393224 | tf_op jit(solution)/shard_map/ppermute | solution.py:263
  16.9 6.2 %collective-permute-start.2 = (bf16[32,2048]{1,0:T(8,128)(2,1)S(1)}, bf16[32,2048]{1,0:T(8,128)(2,1)S(1)}, u32[]{:S(2)}, u32[]{:S(2)}) collective-permute-start(bf16[32,2048]{1,0:T(8,128)(2,1)S(1)} %slice.8), channel_id=1, source_target_pairs={{0,511},{1,480},{2,481},{3,482},{4,483},{5,484},{6,485},{7,486},{8... | collective-permute-start | bytes 393224 | tf_op jit(solution)/shard_map/ppermute | solution.py:263
  23.1 0.1 tile.32
  23.2 0.3 copy.12.down
  23.5 0.6 copy-done.1
  24.1 0.2 tile.34
  24.4 0.2 tile.35.up
  24.5 0.5 copy-done.5
  25.2 0.3 shard_map.91
  25.5 0.7 collective-permute-done.2.refs_3_
  26.2 6.6 %shard_map.92 = (bf16[64,2048]{1,0:T(8,128)(2,1)S(1)}, bf16[32,2048]{1,0:T(8,128)(2,1)S(1)}, bf16[32,2048]{1,0:T(8,128)(2,1)S(1)}) custom-call(s32[5]{0:T(128)S(1)} %stack.43.at, bf16[64,2048]{1,0:T(8,128)(2,1)S(1)} %copy-done, bf16[64,2048]{1,0:T(8,128)(2,1)S(1)} %collective-permute-done.refs_1_, bf16[32,2048]{1,0:T(8,128)(2,1)S(1)} %collective-permute-done.1.refs_2_, ...), custom_call_target="tpu_custom_call" | custom-call | tf_op jit(solution)/shard_map/pallas_call | solution.py:237
  32.9 3.1 %collective-permute-start.4 = (bf16[32,2048]{1,0:T(8,128)(2,1)S(1)}, bf16[32,2048]{1,0:T(8,128)(2,1)S(1)}, u32[]{:S(2)}, u32[]{:S(2)}) collective-permute-start(bf16[32,2048]{1,0:T(8,128)(2,1)S(1)} %get-tuple-element.27), channel_id=1, source_target_pairs={{0,128},{1,129},{2,130},{3,131},{4,132},{5,133},{6,134},{7,135},{8... | collective-permute-start | bytes 393224 | tf_op jit(solution)/shard_map/ppermute | solution.py:263
  36.0 1.9 %collective-permute-start.3 = (bf16[32,2048]{1,0:T(8,128)(2,1)S(1)}, bf16[32,2048]{1,0:T(8,128)(2,1)S(1)}, u32[]{:S(2)}, u32[]{:S(2)}) collective-permute-start(bf16[32,2048]{1,0:T(8,128)(2,1)S(1)} %get-tuple-element.26), channel_id=1, source_target_pairs={{0,0},{1,1},{2,32},{3,33},{4,64},{5,65},{6,96},{7,97},{8,128},{9,1... | collective-permute-start | bytes 393224 | tf_op jit(solution)/shard_map/ppermute | solution.py:263
  37.9 0.8 collective-permute-done.4
  38.7 9.6 %collective-permute-start.5 = (bf16[32,2048]{1,0:T(8,128)(2,1)S(1)}, bf16[32,2048]{1,0:T(8,128)(2,1)S(1)}, u32[]{:S(2)}, u32[]{:S(2)}) collective-permute-start(bf16[32,2048]{1,0:T(8,128)(2,1)S(1)} %collective-permute-done.4), channel_id=1, source_target_pairs={{0,9},{1,8},{2,41},{3,40},{4,73},{5,72},{6,105},{7,104},{8,137},{9... | collective-permute-start | bytes 393224 | tf_op jit(solution)/shard_map/ppermute | solution.py:263
  48.4 0.1 tile.80
  48.5 0.3 copy.13.down
  48.7 0.6 copy-done.2
  49.4 0.2 tile.82
  49.6 0.2 tile.83.up
  49.8 0.3 shard_map.93
  50.0 4.6 %collective-permute-done.5 = bf16[32,2048]{1,0:T(8,128)(2,1)S(1)} collective-permute-done((bf16[32,2048]{1,0:T(8,128)(2,1)S(1)}, bf16[32,2048]{1,0:T(8,128)(2,1)S(1)}, u32[]{:S(2)}, u32[]{:S(2)}) %collective-permute-start.5) | collective-permute-done | bytes 131104 | tf_op jit(solution)/shard_map/ppermute | solution.py:263
  54.7 0.1 multiply_convert_fusion.refs_0_
  54.8 1.9 %collective-permute-start.6 = (bf16[64,2048]{1,0:T(8,128)(2,1)S(1)}, bf16[64,2048]{1,0:T(8,128)(2,1)S(1)}, u32[]{:S(2)}, u32[]{:S(2)}) collective-permute-start(bf16[64,2048]{1,0:T(8,128)(2,1)S(1)} %multiply_convert_fusion.refs_0_), channel_id=1, source_target_pairs={{0,1},{1,2},{2,3},{3,4},{4,5},{5,6},{6,7},{7,8},{8,9},{9,10},{10,1... | collective-permute-start | bytes 786440 | tf_op jit(solution)/shard_map/ppermute | solution.py:263
  56.7 15.5 %collective-permute-start.7 = (bf16[32,2048]{1,0:T(8,128)(2,1)S(1)}, bf16[32,2048]{1,0:T(8,128)(2,1)S(1)}, u32[]{:S(2)}, u32[]{:S(2)}) collective-permute-start(bf16[32,2048]{1,0:T(8,128)(2,1)S(1)} %slice.9), channel_id=1, source_target_pairs={{0,32},{1,33},{2,34},{3,35},{4,36},{5,37},{6,38},{7,39},{8,40},{9,... | collective-permute-start | bytes 393224 | tf_op jit(solution)/shard_map/ppermute | solution.py:263
  72.2 1.9 %collective-permute-start.8 = (bf16[32,2048]{1,0:T(8,128)(2,1)S(1)}, bf16[32,2048]{1,0:T(8,128)(2,1)S(1)}, u32[]{:S(2)}, u32[]{:S(2)}) collective-permute-start(bf16[32,2048]{1,0:T(8,128)(2,1)S(1)} %slice.9), channel_id=1, source_target_pairs={{0,33},{1,34},{2,35},{3,36},{4,37},{5,38},{6,39},{7,40},{8,41},{9,... | collective-permute-start | bytes 393224 | tf_op jit(solution)/shard_map/ppermute | solution.py:263
  74.2 0.7 copy-done.7
  74.9 0.6 copy-done.8
  75.7 5.2 %collective-permute-done.8.refs_3_ = bf16[32,2048]{1,0:T(8,128)(2,1)S(1)} collective-permute-done((bf16[32,2048]{1,0:T(8,128)(2,1)S(1)}, bf16[32,2048]{1,0:T(8,128)(2,1)S(1)}, u32[]{:S(2)}, u32[]{:S(2)}) %collective-permute-start.8) | collective-permute-done | bytes 131104 | tf_op jit(solution)/shard_map/ppermute | solution.py:263
  80.9 6.6 %shard_map.94 = bf16[64,2048]{1,0:T(8,128)(2,1)} custom-call(s32[5]{0:T(128)S(1)} %stack.41.at, bf16[64,2048]{1,0:T(8,128)(2,1)S(1)} %multiply_convert_fusion.refs_0_, bf16[64,2048]{1,0:T(8,128)(2,1)S(1)} %collective-permute-done.6.refs_1_, bf16[32,2048]{1,0:T(8,128)(2,1)S(1)} %collective-permute-done.7.refs_2_, ...), custom_call_target="tpu_custom_call" | custom-call | tf_op jit(solution)/shard_map/pallas_call | solution.py:237
  (29 shorter events, 0.6 us)
Async XLA Ops:
  0.0 23.1 %copy-start.3 = (bf16[2,3,3,32,64]{4,3,2,1,0:T(8,128)(2,1)S(1)}, bf16[2,3,3,32,64]{4,3,2,1,0:T(8,128)(2,1)}, u32[]{:S(2)}) copy-start(bf16[2,3,3,32,64]{4,3,2,1,0:T(8,128)(2,1)} %param.10) | copy-start | bytes 221188
  0.0 26.2 %collective-permute-start = (bf16[64,2048]{1,0:T(8,128)(2,1)}, bf16[64,2048]{1,0:T(8,128)(2,1)S(1)}, u32[]{:S(2)}, u32[]{:S(2)}) collective-permute-start(bf16[64,2048]{1,0:T(8,128)(2,1)} %refs_0_.1), channel_id=1, source_target_pairs={{0,31},{1,0},{2,1},{3,2},{4,3},{5,4},{6,5},{7,6},{8,7},{9,8},{10,9... | collective-permute-start | bytes 786440 | tf_op jit(solution)/shard_map/ppermute | solution.py:263
  14.0 11.5 %collective-permute-start.1 = (bf16[32,2048]{1,0:T(8,128)(2,1)S(1)}, bf16[32,2048]{1,0:T(8,128)(2,1)S(1)}, u32[]{:S(2)}, u32[]{:S(2)}) collective-permute-start(bf16[32,2048]{1,0:T(8,128)(2,1)S(1)} %slice.8), channel_id=1, source_target_pairs={{0,480},{1,481},{2,482},{3,483},{4,484},{5,485},{6,486},{7,487},{8... | collective-permute-start | bytes 393224 | tf_op jit(solution)/shard_map/ppermute | solution.py:263
  16.9 9.4 %collective-permute-start.2 = (bf16[32,2048]{1,0:T(8,128)(2,1)S(1)}, bf16[32,2048]{1,0:T(8,128)(2,1)S(1)}, u32[]{:S(2)}, u32[]{:S(2)}) collective-permute-start(bf16[32,2048]{1,0:T(8,128)(2,1)S(1)} %slice.8), channel_id=1, source_target_pairs={{0,511},{1,480},{2,481},{3,482},{4,483},{5,484},{6,485},{7,486},{8... | collective-permute-start | bytes 393224 | tf_op jit(solution)/shard_map/ppermute | solution.py:263
  23.2 0.9 %copy-start.1 = (bf16[2,3,3,64,32]{3,4,2,1,0:T(8,128)(2,1)S(1)}, bf16[2,3,3,64,32]{3,4,2,1,0:T(8,128)(2,1)}, u32[]{:S(2)}) copy-start(bf16[2,3,3,64,32]{3,4,2,1,0:T(8,128)(2,1)} %param.12) | copy-start | bytes 221188
  24.3 0.7 copy-start.5
  24.3 0.8 copy-start.6
  25.0 1.2 %copy-start = (bf16[64,2048]{1,0:T(8,128)(2,1)S(1)}, bf16[64,2048]{1,0:T(8,128)(2,1)}, u32[]{:S(2)}) copy-start(bf16[64,2048]{1,0:T(8,128)(2,1)} %refs_0_.1) | copy-start | bytes 786436
  26.2 22.1 %copy-start.4 = (bf16[2,3,3,32,64]{4,3,2,1,0:T(8,128)(2,1)S(1)}, bf16[2,3,3,32,64]{4,3,2,1,0:T(8,128)(2,1)}, u32[]{:S(2)}) copy-start(bf16[2,3,3,32,64]{4,3,2,1,0:T(8,128)(2,1)} %param.14) | copy-start | bytes 221188
  32.9 5.8 %collective-permute-start.4 = (bf16[32,2048]{1,0:T(8,128)(2,1)S(1)}, bf16[32,2048]{1,0:T(8,128)(2,1)S(1)}, u32[]{:S(2)}, u32[]{:S(2)}) collective-permute-start(bf16[32,2048]{1,0:T(8,128)(2,1)S(1)} %get-tuple-element.27), channel_id=1, source_target_pairs={{0,128},{1,129},{2,130},{3,131},{4,132},{5,133},{6,134},{7,135},{8... | collective-permute-start | bytes 393224 | tf_op jit(solution)/shard_map/ppermute | solution.py:263
  36.0 14.0 %collective-permute-start.3 = (bf16[32,2048]{1,0:T(8,128)(2,1)S(1)}, bf16[32,2048]{1,0:T(8,128)(2,1)S(1)}, u32[]{:S(2)}, u32[]{:S(2)}) collective-permute-start(bf16[32,2048]{1,0:T(8,128)(2,1)S(1)} %get-tuple-element.26), channel_id=1, source_target_pairs={{0,0},{1,1},{2,32},{3,33},{4,64},{5,65},{6,96},{7,97},{8,128},{9,1... | collective-permute-start | bytes 393224 | tf_op jit(solution)/shard_map/ppermute | solution.py:263
  38.7 16.0 %collective-permute-start.5 = (bf16[32,2048]{1,0:T(8,128)(2,1)S(1)}, bf16[32,2048]{1,0:T(8,128)(2,1)S(1)}, u32[]{:S(2)}, u32[]{:S(2)}) collective-permute-start(bf16[32,2048]{1,0:T(8,128)(2,1)S(1)} %collective-permute-done.4), channel_id=1, source_target_pairs={{0,9},{1,8},{2,41},{3,40},{4,73},{5,72},{6,105},{7,104},{8,137},{9... | collective-permute-start | bytes 393224 | tf_op jit(solution)/shard_map/ppermute | solution.py:263
  48.5 0.9 %copy-start.2 = (bf16[2,3,3,64,32]{3,4,2,1,0:T(8,128)(2,1)S(1)}, bf16[2,3,3,64,32]{3,4,2,1,0:T(8,128)(2,1)}, u32[]{:S(2)}) copy-start(bf16[2,3,3,64,32]{3,4,2,1,0:T(8,128)(2,1)} %param.16) | copy-start | bytes 221188
  54.8 26.2 %collective-permute-start.6 = (bf16[64,2048]{1,0:T(8,128)(2,1)S(1)}, bf16[64,2048]{1,0:T(8,128)(2,1)S(1)}, u32[]{:S(2)}, u32[]{:S(2)}) collective-permute-start(bf16[64,2048]{1,0:T(8,128)(2,1)S(1)} %multiply_convert_fusion.refs_0_), channel_id=1, source_target_pairs={{0,1},{1,2},{2,3},{3,4},{4,5},{5,6},{6,7},{7,8},{8,9},{9,10},{10,1... | collective-permute-start | bytes 786440 | tf_op jit(solution)/shard_map/ppermute | solution.py:263
  56.7 19.0 %collective-permute-start.7 = (bf16[32,2048]{1,0:T(8,128)(2,1)S(1)}, bf16[32,2048]{1,0:T(8,128)(2,1)S(1)}, u32[]{:S(2)}, u32[]{:S(2)}) collective-permute-start(bf16[32,2048]{1,0:T(8,128)(2,1)S(1)} %slice.9), channel_id=1, source_target_pairs={{0,32},{1,33},{2,34},{3,35},{4,36},{5,37},{6,38},{7,39},{8,40},{9,... | collective-permute-start | bytes 393224 | tf_op jit(solution)/shard_map/ppermute | solution.py:263
  72.2 8.7 %collective-permute-start.8 = (bf16[32,2048]{1,0:T(8,128)(2,1)S(1)}, bf16[32,2048]{1,0:T(8,128)(2,1)S(1)}, u32[]{:S(2)}, u32[]{:S(2)}) collective-permute-start(bf16[32,2048]{1,0:T(8,128)(2,1)S(1)} %slice.9), channel_id=1, source_target_pairs={{0,33},{1,34},{2,35},{3,36},{4,37},{5,38},{6,39},{7,40},{8,41},{9,... | collective-permute-start | bytes 393224 | tf_op jit(solution)/shard_map/ppermute | solution.py:263
  74.2 0.7 copy-start.7
  74.9 0.7 copy-start.8

commit v4 on v3

v4 whole, which is shorter than its diff:
```python
import functools

import jax
import jax.numpy as jnp
from jax import lax
from jax.experimental import pallas as pl
from jax.experimental.pallas import tpu as pltpu
from jax.sharding import PartitionSpec as P

ROWS = 64
COLS = 32
CH = 64
HALO = 16
TALL = ROWS + 2 * HALO
MID = 80
F32 = jnp.float32
BF16 = jnp.bfloat16


def lane_group(width, rows):
    return lax.broadcasted_iota(jnp.int32, (rows, 128), 1) // width


def build_weights(down, up, w1, w2, w3, w4):
    by32 = lane_group(32, 64)
    by64 = lane_group(64, 32)
    zero_down = jnp.zeros((64, 128), BF16)
    zero_up = jnp.zeros((32, 128), BF16)
    for p in range(3):
        for i in range(8):
            block = zero_down
            for q in range(3):
                o = i - 1 - q
                if 0 <= o < 4:
                    block = jnp.where(by32 == o, down[0, p, q], block)
            w1[i * 64 : (i + 1) * 64, p * 128 : (p + 1) * 128] = block
        for i in range(8):
            for half in range(2):
                block = zero_up
                for q in range(3):
                    o = i - 2 * q
                    if 0 <= o < 4 and o // 2 == half:
                        block = jnp.where(by64 == o % 2, up[0, p, q], block)
                w2[i * 32 : (i + 1) * 32, half * 384 + p * 128 : half * 384 + p * 128 + 128] = block
        for t in range(4):
            for e in range(2):
                block = zero_down
                for u in range(2):
                    q = t - u
                    if 0 <= q < 3:
                        block = jnp.where(by32 == 2 * u + e, down[1, p, q], block)
                w3[t * 128 + e * 64 : t * 128 + e * 64 + 64, p * 128 : (p + 1) * 128] = block
        for q in range(3):
            for e in range(2):
                block = jnp.where(by64 == e, up[1, p, q], zero_up)
                w4[q * 64 + e * 32 : q * 64 + e * 32 + 32, p * 128 : (p + 1) * 128] = block
        w4[192:256, p * 128 : (p + 1) * 128] = zero_down


def turn_strips(values, halves, row):
    sub = lax.broadcasted_iota(jnp.int32, (8, 128), 0)
    left = lax.broadcasted_iota(jnp.int32, (8, 128), 1) < 64

    def swapped(x, one, other, bit):
        a, b = x[one], x[other]
        low = (sub & bit) == 0
        x[one] = jnp.where(low, a, pltpu.roll(b, bit, 0))
        x[other] = jnp.where(low, pltpu.roll(a, 8 - bit, 0), b)

    for block in range(8):
        x = [values[i][8 * block : 8 * block + 8] for i in range(4)]
        swapped(x, 0, 1, 2)
        swapped(x, 2, 3, 2)
        swapped(x, 0, 2, 4)
        swapped(x, 1, 3, 4)
        for j in range(4):
            z = pltpu.roll(x[j], 64, 1)
            even = jnp.where(left, x[j], pltpu.roll(z, 7, 0))
            odd = jnp.where(left, pltpu.roll(z, 1, 0), x[j])
            both = jnp.where((sub & 1) == 0, even, odd).astype(BF16)
            lane = (4 * block + j) % 16 * 128
            halves[block // 4][row : row + 8, lane : lane + 128] = both


def section_kernel(
    spots, bars, turn, at, *refs
):
    pieces, refs = refs[: len(spots)], refs[len(spots) :]
    w1, w2, w3, w4, down_bias, up_bias, out = refs[:7]
    turning = turn and refs[7:9]
    v, h1, h2, h2_turned = refs[-4:]
    low_on, high_on, cut_low, cut_high = at[0] > 0, at[1] > 0, at[2], at[3]
    low_row, high_row, low_col, high_col = bars

    nothing = jnp.zeros((TALL, 128), BF16)
    v[0] = nothing
    v[33] = nothing
    h1[16] = nothing
    h2[12] = nothing[:MID]
    h2_turned[12] = nothing[:MID]
    for piece, (row, pair) in zip(pieces, spots):
        for i in range(piece.shape[1] // 128):
            v[pair + i + 1, row : row + piece.shape[0], :] = piece[:, i * 128 : (i + 1) * 128]

    sub = lax.broadcasted_iota(jnp.int32, (8, 128), 0)

    def cut(d):
        keep_top = jnp.where((sub >= 8 - d) & (cut_low > 0), 0.0, 1.0)
        keep_low = jnp.where((sub < d) & (cut_high > 0), 0.0, 1.0)
        return keep_top, keep_low

    def wide_dot(chunks, w):
        lhs = jnp.concatenate([jnp.concatenate(c, axis=0) for c in chunks], axis=1)
        return jnp.dot(lhs, w[...], preferred_element_type=F32)

    def masked(x, start, keep):
        pieces = [x[:start], x[start : start + 8] * keep, x[start + 8 :]]
        return jnp.concatenate([p for p in pieces if p.shape[0]], axis=0)

    def parts(part, keep, lo, off):
        top = masked(part[:, lo : lo + 128], low_row - 8 - off, keep[0])
        mid = part[:, lo + 128 : lo + 256]
        low = masked(part[:, lo + 256 : lo + 384], high_row - off, keep[1])
        return top, mid, low

    def taps(res, g, d, keep, lo):
        top, mid, low = parts(res[g * TALL : (g + 1) * TALL], keep, lo, 0)
        return pltpu.roll(top, d, 0) + mid + pltpu.roll(low, TALL - d, 0)

    def below_bar(hit, index, blank):
        return jnp.where(low_on, blank, index) if hit else index

    def above_bar(hit, index, blank):
        return jnp.where(high_on, blank, index) if hit else index

    keep = cut(1)
    for j0 in range(0, 16, 4):
        quads = range(j0, j0 + 4)
        res = wide_dot(
            [
                [v[below_bar(j == 2 * low_col, 2 * j, 33)] for j in quads],
                [v[2 * j + 1] for j in quads],
                [v[2 * j + 2] for j in quads],
                [v[above_bar(j == 2 * high_col - 1, 2 * j + 3, 33)] for j in quads],
            ],
            w1,
        )
        for g, j in enumerate(quads):
            hidden = jnp.maximum(taps(res, g, 1, keep, 0) + down_bias[0:1], 0.0)
            h1[j] = hidden.astype(BF16)

    keep = cut(2)
    steps = []
    for k in range(15):
        near = below_bar(k + 1 == 2 * low_col, k, 16)
        far = above_bar(k + 1 == 2 * high_col, k + 1, 16)
        if k + 1 == 2 * low_col == 2 * high_col:
            steps += [(k, k, far, (0,)), (k, near, k + 1, (1,))]
        else:
            steps.append((k, near, far, (0, 1)))
    for at_step in range(0, len(steps), 4):
        some = steps[at_step : at_step + 4]
        res = wide_dot([[h1[step[1]] for step in some], [h1[step[2]] for step in some]], w2)
        for g, (k, _, _, halves) in enumerate(some):
            for half in halves:
                i = 2 * k + 1 + half
                update = taps(res, g, 2, keep, half * 384) + up_bias[0:1]
                v[i + 1] = (v[i + 1].astype(F32) + update).astype(BF16)

    keep = cut(4)
    for m0 in range(1, 7, 2):
        groups = [(m0 + dm, s) for dm in range(2) for s in range(2)]
        res = wide_dot(
            [
                [v[below_bar(m == low_col, 4 * m + s - 1, 33)] for m, s in groups],
                [v[4 * m + s + 1] for m, s in groups],
                [v[4 * m + s + 3] for m, s in groups],
                [v[above_bar(m == high_col - 1, 4 * m + s + 5, 33)] for m, s in groups],
            ],
            w3,
        )
        for g, (m, s) in enumerate(groups):
            hidden = jnp.maximum(taps(res, g, 4, keep, 0) + down_bias[1:2], 0.0)
            hidden = hidden[8 : 8 + MID]
            h2[2 * (m - 1) + s] = hidden.astype(BF16)
            h2_turned[2 * (m - 1) + s] = pltpu.roll(hidden, 64, 1).astype(BF16)

    keep = cut(8)
    first_half = lax.broadcasted_iota(jnp.int32, (MID, 128), 1) < 64
    for m in range(2, 6):
        groups = [(s, u) for s in range(2) for u in range(2)]
        chunks = [[], []]
        for s, u in groups:
            straight, turned = (h2, h2_turned) if u == 0 else (h2_turned, h2)
            before = below_bar(m == low_col, 2 * (m - 2) + s, 12)
            after = above_bar(m == high_col - 1, 2 * m + s, 12)
            here = 2 * (m - 1) + s
            chunks[0].append(jnp.where(first_half, straight[before], turned[here]))
            chunks[1].append(straight[after])
        res = wide_dot(chunks, w4)
        values = {}
        for g, (s, u) in enumerate(groups):
            top, mid, low = parts(res[g * MID : (g + 1) * MID], keep, 0, 8)
            update = top[0:64] + mid[8:72] + low[16:80] + up_bias[1:2]
            i = 4 * m + s + 2 * u
            value = v[i + 1][HALO : HALO + ROWS].astype(F32) + update
            strip = (i - 8) * 128
            value = value.astype(BF16)
            out[:, strip : strip + 128] = value
            values[s + 2 * u] = value.astype(F32)
        if turn:
            turn_strips(values, turning, 8 * (m - 2))


def weights(down, up):
    vmem = pl.BlockSpec(memory_space=pltpu.VMEM)
    shapes = [(512, 384), (256, 768), (512, 384), (256, 384)]
    return pl.pallas_call(
        build_weights,
        out_shape=[jax.ShapeDtypeStruct(shape, BF16) for shape in shapes],
        in_specs=[vmem, vmem],
        out_specs=[vmem] * 4,
        compiler_params=pltpu.CompilerParams(vmem_limit_bytes=8 << 20),
    )(down, up)


def section(spots, bars, turn, at, pieces, matrices, down_bias, up_bias):
    vmem = pl.BlockSpec(memory_space=pltpu.VMEM)
    out_shape = [jax.ShapeDtypeStruct((ROWS, COLS * CH), BF16)]
    scratch = [
        pltpu.VMEM((34, TALL, 128), BF16),
        pltpu.VMEM((17, TALL, 128), BF16),
        pltpu.VMEM((13, MID, 128), BF16),
        pltpu.VMEM((13, MID, 128), BF16),
    ]
    if turn:
        out_shape += [jax.ShapeDtypeStruct((32, 32 * CH), BF16)] * 2
    return pl.pallas_call(
        functools.partial(section_kernel, spots, bars, turn),
        out_shape=out_shape,
        in_specs=[pl.BlockSpec(memory_space=pltpu.SMEM)] + [vmem] * (len(spots) + 6),
        out_specs=[vmem] * len(out_shape),
        scratch_shapes=scratch,
        compiler_params=pltpu.CompilerParams(vmem_limit_bytes=16 << 20),
    )(at, *pieces, *matrices, down_bias, up_bias)


AHEAD = ((0, 0), (0, 16), (64, 0), (64, 16))
BEHIND = ((32, 16), (32, 0), (0, 16), (0, 0))


def solution(mesh):
    row_count, col_count = mesh.shape["row"], mesh.shape["col"]
    flip = row_count // 4
    axes = ("row", "col")

    def send(x, target):
        pairs = []
        for r in range(row_count):
            for c in range(col_count):
                row, col = target(r, c)
                to = (row % row_count) * col_count + col % col_count
                pairs.append((r * col_count + c, to))
        return lax.ppermute(x, axes, pairs)

    def with_ahead(x):
        corner = send(x[:32], lambda r, c: (r - 1, c - 1))
        right = send(x, lambda r, c: (r, c - 1))
        below = send(x[:32], lambda r, c: (r - 1, c))
        return x, right, below, corner

    def with_behind(x):
        corner = send(x[32:], lambda r, c: (r + 1, c + 1))
        left = send(x, lambda r, c: (r, c + 1))
        above = send(x[32:], lambda r, c: (r + 1, c))
        return x, left, above, corner

    def mirrored(top, bottom, parity):
        near = jnp.where(parity == 0, top, bottom)
        far = jnp.where(parity == 0, bottom, top)
        far = send(far, lambda r, c: (r ^ flip, c))
        near = send(near, lambda r, c: (c // 2, 2 * r + c % 2))
        far = send(far, lambda r, c: (c // 2, 2 * (r ^ flip) + 1 - c % 2))
        even = jnp.concatenate([near, far], axis=0)
        odd = jnp.concatenate([far, near], axis=0)
        return jnp.where(parity == 0, even, odd)

    def per_device(contact, d1, db1, u1, ub1, d2, db2, u2, ub2):
        row, col = lax.axis_index("row"), lax.axis_index("col")
        first_row, last_row = row == 0, row == row_count - 1
        first_col, last_col = col == 0, col == col_count - 1

        def flags(low_at, low_col, high_at, high_col, low_row, high_row):
            return jnp.stack(
                [
                    jnp.where(low_col, low_at, -1),
                    jnp.where(high_col, high_at, -1),
                    low_row.astype(jnp.int32),
                    high_row.astype(jnp.int32),
                ]
            ).astype(jnp.int32)

        def matrices(down, up):
            return weights(
                jnp.tile(down.transpose(0, 1, 2, 4, 3), (1, 1, 1, 1, 4)),
                jnp.tile(up.transpose(0, 1, 2, 4, 3), (1, 1, 1, 1, 2)),
            )

        def biases(down_bias, up_bias):
            return jnp.tile(down_bias, (1, 4)), jnp.tile(up_bias, (1, 2))

        at = flags(4, last_col, 4, last_col, last_row, last_row)
        pieces = with_ahead(contact)
        first, top, bottom = section(
            AHEAD, (64, 64, 4, 4), True, at, pieces, matrices(d1, u1), *biases(db1, ub1)
        )
        later = matrices(d2, u2)
        flipped = mirrored(top, bottom, col % 2)
        symmetric = ((first.astype(F32) + flipped.astype(F32)) * 0.5).astype(BF16)
        symmetric, later = lax.optimization_barrier((symmetric, later))
        at = flags(2, first_col, 6, last_col, first_row, last_row)
        return section(
            BEHIND, (16, 80, 2, 6), False, at, with_behind(symmetric), later, *biases(db2, ub2)
        )[0]

    in_specs = (P("row", "col"), P(), P(), P(), P(), P(), P(), P(), P())
    return jax.shard_map(
        per_device, mesh=mesh, in_specs=in_specs, out_specs=P("row", "col"), check_vma=False
    )
```

time: 88 us -> 81.9 us (0.931)
  Pallas kernels: 13.7 us -> 7.43 us
    pallas_call x2, Pallas kernels: 13.2 us -> 7.01 us  [section(): pl.pallas_call(functools.partial(section_kernel, spots, bars, turn), out_...]
  transfers between devices with their start and end apart: 9 -> 9, of which waited for: 4 -> 4; matrix products, arithmetic and copies ran while one was open for 3% -> 4% of each run, Pallas kernels for 1% -> 1%
where the time goes in v4:
time: 81.9 us; the launch traced here: 81.5 us
  starting transfers between devices  56.3 us (69%)
  waiting for transfers between devices  11.4 us (14%)
  Pallas kernels  7.43 us (9%)
  local copies, waits for them, and re-layouts  5.81 us (7%)
    ppermute x9, starting transfers between devices, send(): return lax.ppermute(x, axes, pairs)  56.3 us
    ppermute x9, waiting for transfers between devices, send(): return lax.ppermute(x, axes, pairs)  11.4 us
    pallas_call x2, Pallas kernels, section(): pl.pallas_call(functools.partial(section_kernel, spots, bars, turn), out_...  7.01 us
    unnamed x18, local copies, waits for them, and re-layouts  3.08 us
  transfers between devices with their start and end apart: 9, of which 4 were waited for; matrix products, arithmetic and copies ran while one was open for 4% of the time, Pallas kernels for 1%

profile of v4, /device:TPU:1, one launch (start us, length us, event | category | flops | bytes accessed | tf_op | source)
XLA Modules:
  0.0 81.5 jit_solution(3640842026803829361)
XLA Ops:
  0.0 13.1 %collective-permute-start = (bf16[64,2048]{1,0:T(8,128)(2,1)}, bf16[64,2048]{1,0:T(8,128)(2,1)S(1)}, u32[]{:S(2)}, u32[]{:S(2)}) collective-permute-start(bf16[64,2048]{1,0:T(8,128)(2,1)} %refs_0_.1), channel_id=1, source_target_pairs={{0,31},{1,0},{2,1},{3,2},{4,3},{5,4},{6,5},{7,6},{8,7},{9,8},{10,9... | collective-permute-start | bytes 786440 | tf_op jit(solution)/shard_map/ppermute | solution.py:264
  13.1 0.9 %slice.8 = bf16[32,2048]{1,0:T(8,128)(2,1)S(1)} slice(bf16[64,2048]{1,0:T(8,128)(2,1)} %refs_0_.1), slice={[0:32], [0:2048]} | slice | bytes 262144 | tf_op jit(solution)/shard_map/slice | solution.py:269
  14.0 2.9 %collective-permute-start.1 = (bf16[32,2048]{1,0:T(8,128)(2,1)S(1)}, bf16[32,2048]{1,0:T(8,128)(2,1)S(1)}, u32[]{:S(2)}, u32[]{:S(2)}) collective-permute-start(bf16[32,2048]{1,0:T(8,128)(2,1)S(1)} %slice.8), channel_id=1, source_target_pairs={{0,480},{1,481},{2,482},{3,483},{4,484},{5,485},{6,486},{7,487},{8... | collective-permute-start | bytes 393224 | tf_op jit(solution)/shard_map/ppermute | solution.py:264
  16.9 6.2 %collective-permute-start.2 = (bf16[32,2048]{1,0:T(8,128)(2,1)S(1)}, bf16[32,2048]{1,0:T(8,128)(2,1)S(1)}, u32[]{:S(2)}, u32[]{:S(2)}) collective-permute-start(bf16[32,2048]{1,0:T(8,128)(2,1)S(1)} %slice.8), channel_id=1, source_target_pairs={{0,511},{1,480},{2,481},{3,482},{4,483},{5,484},{6,485},{7,486},{8... | collective-permute-start | bytes 393224 | tf_op jit(solution)/shard_map/ppermute | solution.py:264
  23.1 0.1 tile.32
  23.2 0.3 copy.12.down
  23.5 0.6 copy-done.1
  24.1 0.2 tile.34
  24.4 0.2 tile.35.up
  24.5 0.5 copy-done.5
  25.2 0.2 shard_map.91
  25.5 0.7 collective-permute-done.2.refs_3_
  26.2 3.2 %shard_map.92 = (bf16[64,2048]{1,0:T(8,128)(2,1)S(1)}, bf16[32,2048]{1,0:T(8,128)(2,1)S(1)}, bf16[32,2048]{1,0:T(8,128)(2,1)S(1)}) custom-call(s32[4]{0:T(128)S(1)} %add_add_fusion.1.at, bf16[64,2048]{1,0:T(8,128)(2,1)S(1)} %copy-done, bf16[64,2048]{1,0:T(8,128)(2,1)S(1)} %collective-permute-done.refs_1_, ...), custom_call_target="tpu_custom_call" | custom-call | tf_op jit(solution)/shard_map/pallas_call | solution.py:238
  29.5 3.3 %collective-permute-start.4 = (bf16[32,2048]{1,0:T(8,128)(2,1)S(1)}, bf16[32,2048]{1,0:T(8,128)(2,1)S(1)}, u32[]{:S(2)}, u32[]{:S(2)}) collective-permute-start(bf16[32,2048]{1,0:T(8,128)(2,1)S(1)} %get-tuple-element.38), channel_id=1, source_target_pairs={{0,128},{1,129},{2,130},{3,131},{4,132},{5,133},{6,134},{7,135},{8... | collective-permute-start | bytes 393224 | tf_op jit(solution)/shard_map/ppermute | solution.py:264
  32.8 1.9 %collective-permute-start.3 = (bf16[32,2048]{1,0:T(8,128)(2,1)S(1)}, bf16[32,2048]{1,0:T(8,128)(2,1)S(1)}, u32[]{:S(2)}, u32[]{:S(2)}) collective-permute-start(bf16[32,2048]{1,0:T(8,128)(2,1)S(1)} %get-tuple-element.37), channel_id=1, source_target_pairs={{0,0},{1,1},{2,32},{3,33},{4,64},{5,65},{6,96},{7,97},{8,128},{9,1... | collective-permute-start | bytes 393224 | tf_op jit(solution)/shard_map/ppermute | solution.py:264
  34.7 0.8 collective-permute-done.4
  35.5 9.7 %collective-permute-start.5 = (bf16[32,2048]{1,0:T(8,128)(2,1)S(1)}, bf16[32,2048]{1,0:T(8,128)(2,1)S(1)}, u32[]{:S(2)}, u32[]{:S(2)}) collective-permute-start(bf16[32,2048]{1,0:T(8,128)(2,1)S(1)} %collective-permute-done.4), channel_id=1, source_target_pairs={{0,9},{1,8},{2,41},{3,40},{4,73},{5,72},{6,105},{7,104},{8,137},{9... | collective-permute-start | bytes 393224 | tf_op jit(solution)/shard_map/ppermute | solution.py:264
  45.1 0.1 tile.80
  45.3 0.3 copy.13.down
  45.5 0.6 copy-done.2
  46.2 0.2 tile.82
  46.4 0.2 tile.83.up
  46.5 0.2 shard_map.93
  46.8 4.7 %collective-permute-done.5 = bf16[32,2048]{1,0:T(8,128)(2,1)S(1)} collective-permute-done((bf16[32,2048]{1,0:T(8,128)(2,1)S(1)}, bf16[32,2048]{1,0:T(8,128)(2,1)S(1)}, u32[]{:S(2)}, u32[]{:S(2)}) %collective-permute-start.5) | collective-permute-done | bytes 131104 | tf_op jit(solution)/shard_map/ppermute | solution.py:264
  51.5 0.1 multiply_convert_fusion.refs_0_
  51.6 1.9 %collective-permute-start.6 = (bf16[64,2048]{1,0:T(8,128)(2,1)S(1)}, bf16[64,2048]{1,0:T(8,128)(2,1)S(1)}, u32[]{:S(2)}, u32[]{:S(2)}) collective-permute-start(bf16[64,2048]{1,0:T(8,128)(2,1)S(1)} %multiply_convert_fusion.refs_0_), channel_id=1, source_target_pairs={{0,1},{1,2},{2,3},{3,4},{4,5},{5,6},{6,7},{7,8},{8,9},{9,10},{10,1... | collective-permute-start | bytes 786440 | tf_op jit(solution)/shard_map/ppermute | solution.py:264
  53.5 15.5 %collective-permute-start.7 = (bf16[32,2048]{1,0:T(8,128)(2,1)S(1)}, bf16[32,2048]{1,0:T(8,128)(2,1)S(1)}, u32[]{:S(2)}, u32[]{:S(2)}) collective-permute-start(bf16[32,2048]{1,0:T(8,128)(2,1)S(1)} %slice.9), channel_id=1, source_target_pairs={{0,32},{1,33},{2,34},{3,35},{4,36},{5,37},{6,38},{7,39},{8,40},{9,... | collective-permute-start | bytes 393224 | tf_op jit(solution)/shard_map/ppermute | solution.py:264
  69.0 1.9 %collective-permute-start.8 = (bf16[32,2048]{1,0:T(8,128)(2,1)S(1)}, bf16[32,2048]{1,0:T(8,128)(2,1)S(1)}, u32[]{:S(2)}, u32[]{:S(2)}) collective-permute-start(bf16[32,2048]{1,0:T(8,128)(2,1)S(1)} %slice.9), channel_id=1, source_target_pairs={{0,33},{1,34},{2,35},{3,36},{4,37},{5,38},{6,39},{7,40},{8,41},{9,... | collective-permute-start | bytes 393224 | tf_op jit(solution)/shard_map/ppermute | solution.py:264
  71.0 0.7 copy-done.7
  71.7 0.6 copy-done.8
  72.5 5.2 %collective-permute-done.8.refs_3_ = bf16[32,2048]{1,0:T(8,128)(2,1)S(1)} collective-permute-done((bf16[32,2048]{1,0:T(8,128)(2,1)S(1)}, bf16[32,2048]{1,0:T(8,128)(2,1)S(1)}, u32[]{:S(2)}, u32[]{:S(2)}) %collective-permute-start.8) | collective-permute-done | bytes 131104 | tf_op jit(solution)/shard_map/ppermute | solution.py:264
  77.7 3.8 %shard_map.94 = bf16[64,2048]{1,0:T(8,128)(2,1)} custom-call(s32[4]{0:T(128)S(1)} %add_add_fusion.at, bf16[64,2048]{1,0:T(8,128)(2,1)S(1)} %multiply_convert_fusion.refs_0_, bf16[64,2048]{1,0:T(8,128)(2,1)S(1)} %collective-permute-done.6.refs_1_, bf16[32,2048]{1,0:T(8,128)(2,1)S(1)} %collective-permute-done.7.refs_2_, ...), custom_call_target="tpu_custom_call" | custom-call | tf_op jit(solution)/shard_map/pallas_call | solution.py:238
  (30 shorter events, 0.6 us)
Async XLA Ops:
  0.0 23.1 %copy-start.3 = (bf16[2,3,3,32,64]{4,3,2,1,0:T(8,128)(2,1)S(1)}, bf16[2,3,3,32,64]{4,3,2,1,0:T(8,128)(2,1)}, u32[]{:S(2)}) copy-start(bf16[2,3,3,32,64]{4,3,2,1,0:T(8,128)(2,1)} %param.10) | copy-start | bytes 221188
  0.0 26.2 %collective-permute-start = (bf16[64,2048]{1,0:T(8,128)(2,1)}, bf16[64,2048]{1,0:T(8,128)(2,1)S(1)}, u32[]{:S(2)}, u32[]{:S(2)}) collective-permute-start(bf16[64,2048]{1,0:T(8,128)(2,1)} %refs_0_.1), channel_id=1, source_target_pairs={{0,31},{1,0},{2,1},{3,2},{4,3},{5,4},{6,5},{7,6},{8,7},{9,8},{10,9... | collective-permute-start | bytes 786440 | tf_op jit(solution)/shard_map/ppermute | solution.py:264
  14.0 11.5 %collective-permute-start.1 = (bf16[32,2048]{1,0:T(8,128)(2,1)S(1)}, bf16[32,2048]{1,0:T(8,128)(2,1)S(1)}, u32[]{:S(2)}, u32[]{:S(2)}) collective-permute-start(bf16[32,2048]{1,0:T(8,128)(2,1)S(1)} %slice.8), channel_id=1, source_target_pairs={{0,480},{1,481},{2,482},{3,483},{4,484},{5,485},{6,486},{7,487},{8... | collective-permute-start | bytes 393224 | tf_op jit(solution)/shard_map/ppermute | solution.py:264
  16.9 9.4 %collective-permute-start.2 = (bf16[32,2048]{1,0:T(8,128)(2,1)S(1)}, bf16[32,2048]{1,0:T(8,128)(2,1)S(1)}, u32[]{:S(2)}, u32[]{:S(2)}) collective-permute-start(bf16[32,2048]{1,0:T(8,128)(2,1)S(1)} %slice.8), channel_id=1, source_target_pairs={{0,511},{1,480},{2,481},{3,482},{4,483},{5,484},{6,485},{7,486},{8... | collective-permute-start | bytes 393224 | tf_op jit(solution)/shard_map/ppermute | solution.py:264
  23.2 0.9 %copy-start.1 = (bf16[2,3,3,64,32]{3,4,2,1,0:T(8,128)(2,1)S(1)}, bf16[2,3,3,64,32]{3,4,2,1,0:T(8,128)(2,1)}, u32[]{:S(2)}) copy-start(bf16[2,3,3,64,32]{3,4,2,1,0:T(8,128)(2,1)} %param.12) | copy-start | bytes 221188
  24.3 0.7 copy-start.5
  24.3 0.8 copy-start.6
  25.0 1.2 %copy-start = (bf16[64,2048]{1,0:T(8,128)(2,1)S(1)}, bf16[64,2048]{1,0:T(8,128)(2,1)}, u32[]{:S(2)}) copy-start(bf16[64,2048]{1,0:T(8,128)(2,1)} %refs_0_.1) | copy-start | bytes 786436
  29.5 15.7 %copy-start.4 = (bf16[2,3,3,32,64]{4,3,2,1,0:T(8,128)(2,1)S(1)}, bf16[2,3,3,32,64]{4,3,2,1,0:T(8,128)(2,1)}, u32[]{:S(2)}) copy-start(bf16[2,3,3,32,64]{4,3,2,1,0:T(8,128)(2,1)} %param.14) | copy-start | bytes 221188
  29.5 5.9 %collective-permute-start.4 = (bf16[32,2048]{1,0:T(8,128)(2,1)S(1)}, bf16[32,2048]{1,0:T(8,128)(2,1)S(1)}, u32[]{:S(2)}, u32[]{:S(2)}) collective-permute-start(bf16[32,2048]{1,0:T(8,128)(2,1)S(1)} %get-tuple-element.38), channel_id=1, source_target_pairs={{0,128},{1,129},{2,130},{3,131},{4,132},{5,133},{6,134},{7,135},{8... | collective-permute-start | bytes 393224 | tf_op jit(solution)/shard_map/ppermute | solution.py:264
  32.8 14.0 %collective-permute-start.3 = (bf16[32,2048]{1,0:T(8,128)(2,1)S(1)}, bf16[32,2048]{1,0:T(8,128)(2,1)S(1)}, u32[]{:S(2)}, u32[]{:S(2)}) collective-permute-start(bf16[32,2048]{1,0:T(8,128)(2,1)S(1)} %get-tuple-element.37), channel_id=1, source_target_pairs={{0,0},{1,1},{2,32},{3,33},{4,64},{5,65},{6,96},{7,97},{8,128},{9,1... | collective-permute-start | bytes 393224 | tf_op jit(solution)/shard_map/ppermute | solution.py:264
  35.5 16.0 %collective-permute-start.5 = (bf16[32,2048]{1,0:T(8,128)(2,1)S(1)}, bf16[32,2048]{1,0:T(8,128)(2,1)S(1)}, u32[]{:S(2)}, u32[]{:S(2)}) collective-permute-start(bf16[32,2048]{1,0:T(8,128)(2,1)S(1)} %collective-permute-done.4), channel_id=1, source_target_pairs={{0,9},{1,8},{2,41},{3,40},{4,73},{5,72},{6,105},{7,104},{8,137},{9... | collective-permute-start | bytes 393224 | tf_op jit(solution)/shard_map/ppermute | solution.py:264
  45.2 0.9 %copy-start.2 = (bf16[2,3,3,64,32]{3,4,2,1,0:T(8,128)(2,1)S(1)}, bf16[2,3,3,64,32]{3,4,2,1,0:T(8,128)(2,1)}, u32[]{:S(2)}) copy-start(bf16[2,3,3,64,32]{3,4,2,1,0:T(8,128)(2,1)} %param.16) | copy-start | bytes 221188
  51.6 26.1 %collective-permute-start.6 = (bf16[64,2048]{1,0:T(8,128)(2,1)S(1)}, bf16[64,2048]{1,0:T(8,128)(2,1)S(1)}, u32[]{:S(2)}, u32[]{:S(2)}) collective-permute-start(bf16[64,2048]{1,0:T(8,128)(2,1)S(1)} %multiply_convert_fusion.refs_0_), channel_id=1, source_target_pairs={{0,1},{1,2},{2,3},{3,4},{4,5},{5,6},{6,7},{7,8},{8,9},{9,10},{10,1... | collective-permute-start | bytes 786440 | tf_op jit(solution)/shard_map/ppermute | solution.py:264
  53.5 19.0 %collective-permute-start.7 = (bf16[32,2048]{1,0:T(8,128)(2,1)S(1)}, bf16[32,2048]{1,0:T(8,128)(2,1)S(1)}, u32[]{:S(2)}, u32[]{:S(2)}) collective-permute-start(bf16[32,2048]{1,0:T(8,128)(2,1)S(1)} %slice.9), channel_id=1, source_target_pairs={{0,32},{1,33},{2,34},{3,35},{4,36},{5,37},{6,38},{7,39},{8,40},{9,... | collective-permute-start | bytes 393224 | tf_op jit(solution)/shard_map/ppermute | solution.py:264
  69.0 8.7 %collective-permute-start.8 = (bf16[32,2048]{1,0:T(8,128)(2,1)S(1)}, bf16[32,2048]{1,0:T(8,128)(2,1)S(1)}, u32[]{:S(2)}, u32[]{:S(2)}) collective-permute-start(bf16[32,2048]{1,0:T(8,128)(2,1)S(1)} %slice.9), channel_id=1, source_target_pairs={{0,33},{1,34},{2,35},{3,36},{4,37},{5,38},{6,39},{7,40},{8,41},{9,... | collective-permute-start | bytes 393224 | tf_op jit(solution)/shard_map/ppermute | solution.py:264
  71.0 0.7 copy-start.7
  71.6 0.7 copy-start.8

commit v5 on v4

--- a/solution.py
+++ b/solution.py
@@ -88,6 +88,9 @@
     pieces, refs = refs[: len(spots)], refs[len(spots) :]
     w1, w2, w3, w4, down_bias, up_bias, out = refs[:7]
     turning = turn and refs[7:9]
+    if not turn:
+        result, out, sent = out, refs[7], refs[8]
+        copies = []
     v, h1, h2, h2_turned = refs[-4:]
     low_on, high_on, cut_low, cut_high = at[0] > 0, at[1] > 0, at[2], at[3]
     low_row, high_row, low_col, high_col = bars
@@ -210,6 +213,16 @@
             values[s + 2 * u] = value.astype(F32)
         if turn:
             turn_strips(values, turning, 8 * (m - 2))
+        else:
+            lanes = slice((m - 2) * 512, (m - 1) * 512)
+            copies.append(
+                pltpu.make_async_copy(out.at[:, lanes], result.at[:, lanes], sent.at[m - 2])
+            )
+            copies[-1].start()
+
+    if not turn:
+        for copy in copies:
+            copy.wait()
 
 
 def weights(down, up):
@@ -235,11 +248,13 @@
     ]
     if turn:
         out_shape += [jax.ShapeDtypeStruct((32, 32 * CH), BF16)] * 2
+    else:
+        scratch = [pltpu.VMEM((ROWS, COLS * CH), BF16), pltpu.SemaphoreType.DMA((4,))] + scratch
     return pl.pallas_call(
         functools.partial(section_kernel, spots, bars, turn),
         out_shape=out_shape,
         in_specs=[pl.BlockSpec(memory_space=pltpu.SMEM)] + [vmem] * (len(spots) + 6),
-        out_specs=[vmem] * len(out_shape),
+        out_specs=[vmem] * 3 if turn else [pl.BlockSpec(memory_space=pl.ANY)],
         scratch_shapes=scratch,
         compiler_params=pltpu.CompilerParams(vmem_limit_bytes=16 << 20),
     )(at, *pieces, *matrices, down_bias, up_bias)

time: 81.9 us -> 81.9 us (level)
  no operation moved by 1% of the time
where the time goes in v5:
time: 81.9 us; the launch traced here: 81.5 us
  starting transfers between devices  56.3 us (69%)
  waiting for transfers between devices  11.4 us (14%)
  Pallas kernels  7.39 us (9%)
  local copies, waits for them, and re-layouts  5.81 us (7%)
    ppermute x9, starting transfers between devices, send(): return lax.ppermute(x, axes, pairs)  56.3 us
    ppermute x9, waiting for transfers between devices, send(): return lax.ppermute(x, axes, pairs)  11.4 us
    pallas_call x2, Pallas kernels, section(): pl.pallas_call(functools.partial(section_kernel, spots, bars, turn), out_...  6.97 us
    unnamed x18, local copies, waits for them, and re-layouts  3.08 us
  transfers between devices with their start and end apart: 9, of which 4 were waited for; matrix products, arithmetic and copies ran while one was open for 4% of the time, Pallas kernels for 1%

profile of v5, /device:TPU:1, one launch (start us, length us, event | category | flops | bytes accessed | tf_op | source)
XLA Modules:
  0.0 81.5 jit_solution(572094575787157167)
XLA Ops:
  0.0 13.1 %collective-permute-start = (bf16[64,2048]{1,0:T(8,128)(2,1)}, bf16[64,2048]{1,0:T(8,128)(2,1)S(1)}, u32[]{:S(2)}, u32[]{:S(2)}) collective-permute-start(bf16[64,2048]{1,0:T(8,128)(2,1)} %refs_0_.1), channel_id=1, source_target_pairs={{0,31},{1,0},{2,1},{3,2},{4,3},{5,4},{6,5},{7,6},{8,7},{9,8},{10,9... | collective-permute-start | bytes 786440 | tf_op jit(solution)/shard_map/ppermute | solution.py:279
  13.1 0.9 %slice.8 = bf16[32,2048]{1,0:T(8,128)(2,1)S(1)} slice(bf16[64,2048]{1,0:T(8,128)(2,1)} %refs_0_.1), slice={[0:32], [0:2048]} | slice | bytes 262144 | tf_op jit(solution)/shard_map/slice | solution.py:284
  14.0 2.9 %collective-permute-start.1 = (bf16[32,2048]{1,0:T(8,128)(2,1)S(1)}, bf16[32,2048]{1,0:T(8,128)(2,1)S(1)}, u32[]{:S(2)}, u32[]{:S(2)}) collective-permute-start(bf16[32,2048]{1,0:T(8,128)(2,1)S(1)} %slice.8), channel_id=1, source_target_pairs={{0,480},{1,481},{2,482},{3,483},{4,484},{5,485},{6,486},{7,487},{8... | collective-permute-start | bytes 393224 | tf_op jit(solution)/shard_map/ppermute | solution.py:279
  16.9 6.2 %collective-permute-start.2 = (bf16[32,2048]{1,0:T(8,128)(2,1)S(1)}, bf16[32,2048]{1,0:T(8,128)(2,1)S(1)}, u32[]{:S(2)}, u32[]{:S(2)}) collective-permute-start(bf16[32,2048]{1,0:T(8,128)(2,1)S(1)} %slice.8), channel_id=1, source_target_pairs={{0,511},{1,480},{2,481},{3,482},{4,483},{5,484},{6,485},{7,486},{8... | collective-permute-start | bytes 393224 | tf_op jit(solution)/shard_map/ppermute | solution.py:279
  23.1 0.1 tile.32
  23.2 0.3 copy.12.down
  23.5 0.6 copy-done.1
  24.1 0.2 tile.34
  24.4 0.2 tile.35.up
  24.5 0.5 copy-done.5
  25.2 0.2 shard_map.91
  25.5 0.7 collective-permute-done.2.refs_3_
  26.2 3.2 %shard_map.92 = (bf16[64,2048]{1,0:T(8,128)(2,1)S(1)}, bf16[32,2048]{1,0:T(8,128)(2,1)S(1)}, bf16[32,2048]{1,0:T(8,128)(2,1)S(1)}) custom-call(s32[4]{0:T(128)S(1)} %add_add_fusion.1.at, bf16[64,2048]{1,0:T(8,128)(2,1)S(1)} %copy-done, bf16[64,2048]{1,0:T(8,128)(2,1)S(1)} %collective-permute-done.refs_1_, ...), custom_call_target="tpu_custom_call" | custom-call | tf_op jit(solution)/shard_map/pallas_call | solution.py:253
  29.5 3.3 %collective-permute-start.4 = (bf16[32,2048]{1,0:T(8,128)(2,1)S(1)}, bf16[32,2048]{1,0:T(8,128)(2,1)S(1)}, u32[]{:S(2)}, u32[]{:S(2)}) collective-permute-start(bf16[32,2048]{1,0:T(8,128)(2,1)S(1)} %get-tuple-element.38), channel_id=1, source_target_pairs={{0,128},{1,129},{2,130},{3,131},{4,132},{5,133},{6,134},{7,135},{8... | collective-permute-start | bytes 393224 | tf_op jit(solution)/shard_map/ppermute | solution.py:279
  32.8 1.9 %collective-permute-start.3 = (bf16[32,2048]{1,0:T(8,128)(2,1)S(1)}, bf16[32,2048]{1,0:T(8,128)(2,1)S(1)}, u32[]{:S(2)}, u32[]{:S(2)}) collective-permute-start(bf16[32,2048]{1,0:T(8,128)(2,1)S(1)} %get-tuple-element.37), channel_id=1, source_target_pairs={{0,0},{1,1},{2,32},{3,33},{4,64},{5,65},{6,96},{7,97},{8,128},{9,1... | collective-permute-start | bytes 393224 | tf_op jit(solution)/shard_map/ppermute | solution.py:279
  34.7 0.8 collective-permute-done.4
  35.5 9.7 %collective-permute-start.5 = (bf16[32,2048]{1,0:T(8,128)(2,1)S(1)}, bf16[32,2048]{1,0:T(8,128)(2,1)S(1)}, u32[]{:S(2)}, u32[]{:S(2)}) collective-permute-start(bf16[32,2048]{1,0:T(8,128)(2,1)S(1)} %collective-permute-done.4), channel_id=1, source_target_pairs={{0,9},{1,8},{2,41},{3,40},{4,73},{5,72},{6,105},{7,104},{8,137},{9... | collective-permute-start | bytes 393224 | tf_op jit(solution)/shard_map/ppermute | solution.py:279
  45.1 0.1 tile.80
  45.3 0.3 copy.13.down
  45.5 0.6 copy-done.2
  46.2 0.2 tile.82
  46.4 0.2 tile.83.up
  46.5 0.2 shard_map.93
  46.8 4.7 %collective-permute-done.5 = bf16[32,2048]{1,0:T(8,128)(2,1)S(1)} collective-permute-done((bf16[32,2048]{1,0:T(8,128)(2,1)S(1)}, bf16[32,2048]{1,0:T(8,128)(2,1)S(1)}, u32[]{:S(2)}, u32[]{:S(2)}) %collective-permute-start.5) | collective-permute-done | bytes 131104 | tf_op jit(solution)/shard_map/ppermute | solution.py:279
  51.5 0.1 multiply_convert_fusion.refs_0_
  51.6 1.9 %collective-permute-start.6 = (bf16[64,2048]{1,0:T(8,128)(2,1)S(1)}, bf16[64,2048]{1,0:T(8,128)(2,1)S(1)}, u32[]{:S(2)}, u32[]{:S(2)}) collective-permute-start(bf16[64,2048]{1,0:T(8,128)(2,1)S(1)} %multiply_convert_fusion.refs_0_), channel_id=1, source_target_pairs={{0,1},{1,2},{2,3},{3,4},{4,5},{5,6},{6,7},{7,8},{8,9},{9,10},{10,1... | collective-permute-start | bytes 786440 | tf_op jit(solution)/shard_map/ppermute | solution.py:279
  53.5 15.5 %collective-permute-start.7 = (bf16[32,2048]{1,0:T(8,128)(2,1)S(1)}, bf16[32,2048]{1,0:T(8,128)(2,1)S(1)}, u32[]{:S(2)}, u32[]{:S(2)}) collective-permute-start(bf16[32,2048]{1,0:T(8,128)(2,1)S(1)} %slice.9), channel_id=1, source_target_pairs={{0,32},{1,33},{2,34},{3,35},{4,36},{5,37},{6,38},{7,39},{8,40},{9,... | collective-permute-start | bytes 393224 | tf_op jit(solution)/shard_map/ppermute | solution.py:279
  69.0 1.9 %collective-permute-start.8 = (bf16[32,2048]{1,0:T(8,128)(2,1)S(1)}, bf16[32,2048]{1,0:T(8,128)(2,1)S(1)}, u32[]{:S(2)}, u32[]{:S(2)}) collective-permute-start(bf16[32,2048]{1,0:T(8,128)(2,1)S(1)} %slice.9), channel_id=1, source_target_pairs={{0,33},{1,34},{2,35},{3,36},{4,37},{5,38},{6,39},{7,40},{8,41},{9,... | collective-permute-start | bytes 393224 | tf_op jit(solution)/shard_map/ppermute | solution.py:279
  71.0 0.7 copy-done.7
  71.7 0.6 copy-done.8
  72.5 5.2 %collective-permute-done.8.refs_3_ = bf16[32,2048]{1,0:T(8,128)(2,1)S(1)} collective-permute-done((bf16[32,2048]{1,0:T(8,128)(2,1)S(1)}, bf16[32,2048]{1,0:T(8,128)(2,1)S(1)}, u32[]{:S(2)}, u32[]{:S(2)}) %collective-permute-start.8) | collective-permute-done | bytes 131104 | tf_op jit(solution)/shard_map/ppermute | solution.py:279
  77.7 3.8 %shard_map.94 = bf16[64,2048]{1,0:T(8,128)(2,1)} custom-call(s32[4]{0:T(128)S(1)} %add_add_fusion.at, bf16[64,2048]{1,0:T(8,128)(2,1)S(1)} %multiply_convert_fusion.refs_0_, bf16[64,2048]{1,0:T(8,128)(2,1)S(1)} %collective-permute-done.6.refs_1_, bf16[32,2048]{1,0:T(8,128)(2,1)S(1)} %collective-permute-done.7.refs_2_, ...), custom_call_target="tpu_custom_call" | custom-call | tf_op jit(solution)/shard_map/pallas_call | solution.py:253
  (30 shorter events, 0.6 us)
Async XLA Ops:
  0.0 23.1 %copy-start.3 = (bf16[2,3,3,32,64]{4,3,2,1,0:T(8,128)(2,1)S(1)}, bf16[2,3,3,32,64]{4,3,2,1,0:T(8,128)(2,1)}, u32[]{:S(2)}) copy-start(bf16[2,3,3,32,64]{4,3,2,1,0:T(8,128)(2,1)} %param.10) | copy-start | bytes 221188
  0.0 26.2 %collective-permute-start = (bf16[64,2048]{1,0:T(8,128)(2,1)}, bf16[64,2048]{1,0:T(8,128)(2,1)S(1)}, u32[]{:S(2)}, u32[]{:S(2)}) collective-permute-start(bf16[64,2048]{1,0:T(8,128)(2,1)} %refs_0_.1), channel_id=1, source_target_pairs={{0,31},{1,0},{2,1},{3,2},{4,3},{5,4},{6,5},{7,6},{8,7},{9,8},{10,9... | collective-permute-start | bytes 786440 | tf_op jit(solution)/shard_map/ppermute | solution.py:279
  14.0 11.5 %collective-permute-start.1 = (bf16[32,2048]{1,0:T(8,128)(2,1)S(1)}, bf16[32,2048]{1,0:T(8,128)(2,1)S(1)}, u32[]{:S(2)}, u32[]{:S(2)}) collective-permute-start(bf16[32,2048]{1,0:T(8,128)(2,1)S(1)} %slice.8), channel_id=1, source_target_pairs={{0,480},{1,481},{2,482},{3,483},{4,484},{5,485},{6,486},{7,487},{8... | collective-permute-start | bytes 393224 | tf_op jit(solution)/shard_map/ppermute | solution.py:279
  16.9 9.4 %collective-permute-start.2 = (bf16[32,2048]{1,0:T(8,128)(2,1)S(1)}, bf16[32,2048]{1,0:T(8,128)(2,1)S(1)}, u32[]{:S(2)}, u32[]{:S(2)}) collective-permute-start(bf16[32,2048]{1,0:T(8,128)(2,1)S(1)} %slice.8), channel_id=1, source_target_pairs={{0,511},{1,480},{2,481},{3,482},{4,483},{5,484},{6,485},{7,486},{8... | collective-permute-start | bytes 393224 | tf_op jit(solution)/shard_map/ppermute | solution.py:279
  23.2 0.9 %copy-start.1 = (bf16[2,3,3,64,32]{3,4,2,1,0:T(8,128)(2,1)S(1)}, bf16[2,3,3,64,32]{3,4,2,1,0:T(8,128)(2,1)}, u32[]{:S(2)}) copy-start(bf16[2,3,3,64,32]{3,4,2,1,0:T(8,128)(2,1)} %param.12) | copy-start | bytes 221188
  24.3 0.7 copy-start.5
  24.3 0.8 copy-start.6
  25.0 1.2 %copy-start = (bf16[64,2048]{1,0:T(8,128)(2,1)S(1)}, bf16[64,2048]{1,0:T(8,128)(2,1)}, u32[]{:S(2)}) copy-start(bf16[64,2048]{1,0:T(8,128)(2,1)} %refs_0_.1) | copy-start | bytes 786436
  29.5 15.7 %copy-start.4 = (bf16[2,3,3,32,64]{4,3,2,1,0:T(8,128)(2,1)S(1)}, bf16[2,3,3,32,64]{4,3,2,1,0:T(8,128)(2,1)}, u32[]{:S(2)}) copy-start(bf16[2,3,3,32,64]{4,3,2,1,0:T(8,128)(2,1)} %param.14) | copy-start | bytes 221188
  29.5 5.9 %collective-permute-start.4 = (bf16[32,2048]{1,0:T(8,128)(2,1)S(1)}, bf16[32,2048]{1,0:T(8,128)(2,1)S(1)}, u32[]{:S(2)}, u32[]{:S(2)}) collective-permute-start(bf16[32,2048]{1,0:T(8,128)(2,1)S(1)} %get-tuple-element.38), channel_id=1, source_target_pairs={{0,128},{1,129},{2,130},{3,131},{4,132},{5,133},{6,134},{7,135},{8... | collective-permute-start | bytes 393224 | tf_op jit(solution)/shard_map/ppermute | solution.py:279
  32.8 14.0 %collective-permute-start.3 = (bf16[32,2048]{1,0:T(8,128)(2,1)S(1)}, bf16[32,2048]{1,0:T(8,128)(2,1)S(1)}, u32[]{:S(2)}, u32[]{:S(2)}) collective-permute-start(bf16[32,2048]{1,0:T(8,128)(2,1)S(1)} %get-tuple-element.37), channel_id=1, source_target_pairs={{0,0},{1,1},{2,32},{3,33},{4,64},{5,65},{6,96},{7,97},{8,128},{9,1... | collective-permute-start | bytes 393224 | tf_op jit(solution)/shard_map/ppermute | solution.py:279
  35.5 16.0 %collective-permute-start.5 = (bf16[32,2048]{1,0:T(8,128)(2,1)S(1)}, bf16[32,2048]{1,0:T(8,128)(2,1)S(1)}, u32[]{:S(2)}, u32[]{:S(2)}) collective-permute-start(bf16[32,2048]{1,0:T(8,128)(2,1)S(1)} %collective-permute-done.4), channel_id=1, source_target_pairs={{0,9},{1,8},{2,41},{3,40},{4,73},{5,72},{6,105},{7,104},{8,137},{9... | collective-permute-start | bytes 393224 | tf_op jit(solution)/shard_map/ppermute | solution.py:279
  45.2 0.9 %copy-start.2 = (bf16[2,3,3,64,32]{3,4,2,1,0:T(8,128)(2,1)S(1)}, bf16[2,3,3,64,32]{3,4,2,1,0:T(8,128)(2,1)}, u32[]{:S(2)}) copy-start(bf16[2,3,3,64,32]{3,4,2,1,0:T(8,128)(2,1)} %param.16) | copy-start | bytes 221188
  51.6 26.1 %collective-permute-start.6 = (bf16[64,2048]{1,0:T(8,128)(2,1)S(1)}, bf16[64,2048]{1,0:T(8,128)(2,1)S(1)}, u32[]{:S(2)}, u32[]{:S(2)}) collective-permute-start(bf16[64,2048]{1,0:T(8,128)(2,1)S(1)} %multiply_convert_fusion.refs_0_), channel_id=1, source_target_pairs={{0,1},{1,2},{2,3},{3,4},{4,5},{5,6},{6,7},{7,8},{8,9},{9,10},{10,1... | collective-permute-start | bytes 786440 | tf_op jit(solution)/shard_map/ppermute | solution.py:279
  53.5 19.0 %collective-permute-start.7 = (bf16[32,2048]{1,0:T(8,128)(2,1)S(1)}, bf16[32,2048]{1,0:T(8,128)(2,1)S(1)}, u32[]{:S(2)}, u32[]{:S(2)}) collective-permute-start(bf16[32,2048]{1,0:T(8,128)(2,1)S(1)} %slice.9), channel_id=1, source_target_pairs={{0,32},{1,33},{2,34},{3,35},{4,36},{5,37},{6,38},{7,39},{8,40},{9,... | collective-permute-start | bytes 393224 | tf_op jit(solution)/shard_map/ppermute | solution.py:279
  69.0 8.7 %collective-permute-start.8 = (bf16[32,2048]{1,0:T(8,128)(2,1)S(1)}, bf16[32,2048]{1,0:T(8,128)(2,1)S(1)}, u32[]{:S(2)}, u32[]{:S(2)}) collective-permute-start(bf16[32,2048]{1,0:T(8,128)(2,1)S(1)} %slice.9), channel_id=1, source_target_pairs={{0,33},{1,34},{2,35},{3,36},{4,37},{5,38},{6,39},{7,40},{8,41},{9,... | collective-permute-start | bytes 393224 | tf_op jit(solution)/shard_map/ppermute | solution.py:279
  71.0 0.7 copy-start.7
  71.6 0.7 copy-start.8
